TPU v7x, 256 devices: a whole 4x4x8 slice. The times are simulated.
256 devices in a mesh: event: 4 (over z_lo, core), space: 64 (over x, z_hi, y).
Axes of the slice: x: 4, y: 4, z: 8 (z_hi: 4, z_lo: 2; z = z_hi * 2 + z_lo), core: 2. Of those that a mesh axis runs over, the one named last changes fastest.
Arguments:
- state_now: float32 [4, 512, 16, 512], P('event', 'space'), may hold values from -6 to 6
- state_prev: float32 [4, 512, 16, 512], P('event', 'space'), may hold values from -6 to 6
- adjoint_now: float32 [4, 512, 16, 512], P('event', 'space'), may hold values from -1.8 to 1.8
- adjoint_next: float32 [4, 512, 16, 512], P('event', 'space'), may hold values from -1.8 to 1.8
- modulus: float32 [5, 128, 5, 4, 5, 128], P(None, 'space'), may hold values from 0.5 to 2
- density: float32 [512, 16, 512], P('space'), may hold values from 0.5 to 2
- receivers: int32 [8192], P('space'), may hold values from 0 to 65535
- observed: float32 [4, 3, 8192], P('event', None, 'space'), may hold values from -12 to 12
Outputs:
- kernel: float32 [5, 128, 5, 4, 5, 128], P(None, 'space', None, 'event')
- misfit: float32 [4], P('event')
Inputs may be any that keep to these rules, and one draw needn't show every extreme that they name: A node of the receiver's own slab, numbered with the third index fastest over 8 x 16 x 512 nodes; two receivers may share a node.
All inputs are finite; a program needn't handle non-finite values. Where the computation divides by a largest or mean magnitude, that divisor is 1e-20 or more.
Results may differ from a plain program's by a relative error of at most 0.00011.
Values sent between devices are 32-bit elements; how exact they have to be, the bound alone decides.
No kernel may reach another device: no remote copies, remote signals or barrier semaphores. Data moves between devices by JAX's collectives and lax.ppermute only.
A program may use at most 64 MiB of HBM per device.

v0:
```python
import math

import jax
import jax.numpy as jnp
import numpy as np
from jax import lax
from jax.experimental import pallas as pl
from jax.experimental.pallas import tpu as pltpu
from jax.sharding import PartitionSpec as P


TIME_STEP = 0.05
EPSILON = 1e-06
F32 = jnp.float32
BF16 = jnp.bfloat16
SAMPLES = 24576


def gll_tables():
    root = math.sqrt(3.0 / 7.0)
    points = np.array([-1.0, -root, 0.0, root, 1.0])
    weights = np.array([0.1, 49.0 / 90.0, 32.0 / 45.0, 49.0 / 90.0, 0.1])
    legendre = (35.0 * points**4 - 30.0 * points**2 + 3.0) / 8.0
    derivative = np.zeros((5, 5))
    for row in range(5):
        for column in range(5):
            if row != column:
                derivative[row, column] = legendre[row] / (
                    legendre[column] * (points[row] - points[column])
                )
    derivative[0, 0] = -5.0
    derivative[4, 4] = 5.0
    return derivative, weights


DERIVATIVE, WEIGHTS = gll_tables()


def apply_line(matrix, u):
    e0, e1 = u[0] + u[4], u[1] + u[3]
    o0, o1 = u[0] - u[4], u[1] - u[3]
    out = [None] * 5
    for s in (0, 1):
        m = matrix[s]
        plus = float(0.5 * (m[0] - m[4])) * o0 + float(0.5 * (m[1] - m[3])) * o1
        minus = (
            float(0.5 * (m[0] + m[4])) * e0
            + float(0.5 * (m[1] + m[3])) * e1
            + float(m[2]) * u[2]
        )
        out[s] = plus + minus
        out[4 - s] = plus - minus
    out[2] = float(matrix[2][0]) * o0 + float(matrix[2][1]) * o1
    return out


def forward_line(u):
    return apply_line(DERIVATIVE, u)


def backward_line(h):
    return apply_line(DERIVATIVE.T, h)


def iotas():
    sub = lax.broadcasted_iota(jnp.int32, (8, 128), 0)
    lane = lax.broadcasted_iota(jnp.int32, (8, 128), 1)
    return sub, lane


def half_turn(v):
    return pltpu.roll(v, 4, 0)


class Shifts:
    def __init__(self):
        sub, lane = iotas()
        self.low = sub < 4
        self.row_first = (sub % 4) == 0
        self.row_last = (sub % 4) == 3
        self.lane_first = lane == 0
        self.lane_last = lane == 127

    def next_y(self, v):
        return jnp.where(self.row_last, 0.0, pltpu.roll(v, 7, 0))

    def next_z(self, v):
        return jnp.where(self.lane_last, 0.0, pltpu.roll(v, 127, 1))

    def carry_y(self, v):
        return jnp.where(self.row_first, 0.0, pltpu.roll(v, 1, 0))

    def carry_z(self, v):
        return jnp.where(self.lane_first, 0.0, pltpu.roll(v, 1, 1))


def pack_low(sh, halves):
    return [
        jnp.where(sh.low, halves[2 * k], half_turn(halves[2 * k + 1])) for k in range(8)
    ]


def pack_high(sh, halves):
    return [
        jnp.where(sh.low, half_turn(halves[2 * k]), halves[2 * k + 1]) for k in range(8)
    ]


def to_high(ref, base, qr):
    v = ref[base + qr // 2]
    return half_turn(v) if qr % 2 == 0 else v


def extended(sh, field, message, base):
    def get(p, qr):
        if p < 4:
            return field[p * 16 + qr]
        return jnp.where(sh.low, half_turn(field[qr]), to_high(message, base, qr))

    return get


def stored(field):
    def get(p, qr):
        return field[p * 16 + qr]

    return get


def expand(sh, get, blocks):
    for p in range(5):
        for r in range(4):
            for q in range(4):
                v = get(p, q * 4 + r)
                blocks[p * 25 + q * 5 + r] = v
                if r == 0:
                    blocks[p * 25 + q * 5 + 4] = sh.next_z(v)
                if q == 0:
                    far = sh.next_y(v)
                    blocks[p * 25 + 20 + r] = far
                    if r == 0:
                        blocks[p * 25 + 24] = sh.next_z(far)


def line_indices(direction, a, b):
    if direction == 0:
        return [k * 25 + a * 5 + b for k in range(5)]
    if direction == 1:
        return [a * 25 + k * 5 + b for k in range(5)]
    return [a * 25 + b * 5 + k for k in range(5)]


def force(sh, blocks, stiff, scratch, out):
    for q in range(5):
        for r in range(5):
            at = line_indices(0, q, r)
            g = forward_line([blocks[i] for i in at])
            f = backward_line([stiff[i] * g[k] for k, i in enumerate(at)])
            for k, i in enumerate(at):
                scratch[i] = f[k]
    for p in range(5):
        total = {}
        for q in range(5):
            at = line_indices(2, p, q)
            g = forward_line([blocks[i] for i in at])
            f = backward_line([stiff[i] * g[k] for k, i in enumerate(at)])
            for k, i in enumerate(at):
                total[i] = scratch[i] + f[k]
        for r in range(5):
            at = line_indices(1, p, r)
            g = forward_line([blocks[i] for i in at])
            f = backward_line([stiff[i] * g[k] for k, i in enumerate(at)])
            for k, i in enumerate(at):
                total[i] = total[i] + f[k]
        for qr, v in enumerate(assemble(sh, [total[p * 25 + n] for n in range(25)])):
            out[p * 16 + qr] = v


def assemble(sh, face):
    rows = {}
    for q in range(5):
        rows[q, 0] = face[q * 5] + sh.carry_z(face[q * 5 + 4])
        for r in range(1, 4):
            rows[q, r] = face[q * 5 + r]
    nodes = []
    for q in range(4):
        for r in range(4):
            nodes.append(rows[0, r] + sh.carry_y(rows[4, r]) if q == 0 else rows[q, r])
    return nodes


def products(first, second, acc, initial):
    for direction in range(3):
        for a in range(5):
            for b in range(5):
                at = line_indices(direction, a, b)
                g = forward_line([first[i] for i in at])
                h = forward_line([second[i] for i in at])
                for k, i in enumerate(at):
                    if initial and direction == 0:
                        acc[i] = g[k] * h[k]
                    else:
                        acc[i] = acc[i] + g[k] * h[k]


def assembled(sh, forces, incoming, base):
    def total(p, qr):
        f = forces[p * 16 + qr]
        if p == 0:
            return f + jnp.where(
                sh.low, incoming.from_left(base, qr), half_turn(forces[64 + qr])
            )
        if p == 4:
            return f + jnp.where(
                sh.low, half_turn(forces[qr]), incoming.from_right(base, qr)
            )
        return f

    return total


def put_messages(sh, odd, forces, far, near, base):
    to_left = pack_low(sh, [forces[qr] for qr in range(16)])
    to_right = pack_high(sh, [forces[64 + qr] for qr in range(16)])
    for k in range(8):
        far[base + k] = jnp.where(odd, to_right[k], to_left[k])
        near[base + k] = jnp.where(odd, to_left[k], to_right[k])


class Incoming:
    def __init__(self, odd, far, near):
        self.odd, self.far, self.near = odd, far, near

    def from_left(self, base, qr):
        at = base + qr // 2
        v = jnp.where(self.odd, self.near[at], self.far[at])
        return v if qr % 2 == 0 else half_turn(v)

    def from_right(self, base, qr):
        at = base + qr // 2
        v = jnp.where(self.odd, self.far[at], self.near[at])
        return half_turn(v) if qr % 2 == 0 else v


def is_odd(slab_ref):
    return slab_ref[0] % 2 == 1


def split3(x):
    hi = x.astype(BF16)
    rest = x - hi.astype(F32)
    mid = rest.astype(BF16)
    lo = (rest - mid.astype(F32)).astype(BF16)
    return hi, mid, lo


def selection(swap):
    z = lax.broadcasted_iota(jnp.int32, (256, 256), 0)
    c = lax.broadcasted_iota(jnp.int32, (256, 256), 1)
    r = c // 64
    if swap:
        r = r + 1 - 2 * (r % 2)
    return jnp.where(z == 4 * (c % 64) + r, 1.0, 0.0).astype(BF16)


def to_local(x_ref, near, far, rows, emit):
    x = jnp.concatenate([x_ref[4 * i + p] for p in range(4) for i in range(2)], axis=0)
    first = second = None
    for part in split3(x):
        a = jnp.dot(part[:, :256], near, preferred_element_type=F32)
        b = jnp.dot(part[:, 256:], far, preferred_element_type=F32)
        first = a if first is None else first + a
        second = b if second is None else second + b
    lower = lax.broadcasted_iota(jnp.int32, (128, 128), 1) < 64
    for half in range(2):
        a = first[:, 128 * half : 128 * half + 128]
        b = second[:, 128 * half : 128 * half + 128]
        rows[2 * half] = jnp.where(lower, a, b)
        rows[2 * half + 1] = pltpu.roll(jnp.where(lower, b, a), 64, 1)
    for p in range(4):
        for q in range(4):
            for r in range(4):
                emit(p, q * 4 + r, rows[r, pl.ds(32 * p + q, 8, stride=4), :])


def load(sources, buffers, semaphores):
    copies = [
        pltpu.make_async_copy(source, buffer, semaphores.at[k])
        for k, (source, buffer) in enumerate(zip(sources, buffers))
    ]
    for copy in copies:
        copy.start()
    return copies


def first_kernel(
    now_hbm, adjoint_hbm, u_out, lam_out, message, rows, now_ref, adjoint_ref, semaphores
):
    copies = load((now_hbm, adjoint_hbm), (now_ref, adjoint_ref), semaphores)
    sh = Shifts()
    near, far = selection(False), selection(True)
    for which, (source, target) in enumerate(((now_ref, u_out), (adjoint_ref, lam_out))):

        def emit(p, qr, v, target=target):
            target[p * 16 + qr] = v

        copies[which].wait()
        to_local(source, near, far, rows, emit)
        for k, v in enumerate(pack_low(sh, [target[qr] for qr in range(16)])):
            message[8 * which + k] = v


def receiver_rows(receivers):
    x, yz = receivers // 8192, receivers % 8192
    y, z = yz // 512, yz % 512
    i, p, j, q, r = x // 4, x % 4, y // 4, y % 4, z % 4
    return ((p * 4 + q) * 4 + r) * 8 + i * 4 + j, z // 4


def one_hots(receivers):
    row, lane = receiver_rows(receivers)
    row_hot = lax.broadcasted_iota(jnp.int32, (512, 128), 0) == row
    lane_hot = lax.broadcasted_iota(jnp.int32, (128, 128), 0) == lane
    return row_hot, lane_hot


def second_kernel(
    slab_ref,
    prev_hbm,
    next_hbm,
    density_hbm,
    modulus_hbm,
    receivers_ref,
    observed_ref,
    prev_out,
    next_out,
    scale_out,
    stiff_out,
    counts_out,
    message,
    rows,
    prev_ref,
    next_ref,
    density_ref,
    modulus_ref,
    semaphores,
):
    copies = load(
        (prev_hbm, next_hbm, density_hbm, modulus_hbm),
        (prev_ref, next_ref, density_ref, modulus_ref),
        semaphores,
    )
    sh = Shifts()
    sub, lane = iotas()
    near, far = selection(False), selection(True)
    for which, (source, target) in enumerate(((prev_ref, prev_out), (next_ref, next_out))):

        def emit(p, qr, v, target=target):
            target[p * 16 + qr] = v

        copies[which].wait()
        to_local(source, near, far, rows, emit)
    line = (0.2, 49.0 / 90.0, 32.0 / 45.0, 49.0 / 90.0)
    first_x = jnp.logical_and(sh.low, slab_ref[0] == 0)

    def emit_scale(p, qr, v):
        q, r = qr // 4, qr % 4
        mass = v * (jnp.where(first_x, 0.1, 0.2).astype(F32) if p == 0 else line[p])
        mass = mass * (jnp.where(sh.row_first, 0.1, 0.2).astype(F32) if q == 0 else line[q])
        mass = mass * (jnp.where(sh.lane_first, 0.1, 0.2).astype(F32) if r == 0 else line[r])
        scale_out[p * 16 + qr] = (TIME_STEP * TIME_STEP) / mass

    copies[2].wait()
    to_local(density_ref, near, far, rows, emit_scale)
    copies[3].wait()
    for p in range(5):
        for q in range(5):
            for r in range(5):
                weight = float(WEIGHTS[p] * WEIGHTS[q] * WEIGHTS[r])
                block = jnp.concatenate(
                    [modulus_ref[p, 0, q, r], modulus_ref[p, 1, q, r]], axis=0
                )
                stiff_out[p * 25 + q * 5 + r] = weight * block
    row_hot, lane_hot = one_hots(receivers_ref[...])
    row_hot = jnp.where(row_hot, 1.0, 0.0).astype(BF16)
    ones = jnp.where(lane_hot, 1.0, 0.0)
    contract = (((1,), (1,)), ((), ()))

    def put_counts(which, total):
        for n in range(64):
            counts_out[which * 64 + n] = total[8 * n : 8 * n + 8]

    put_counts(
        0, lax.dot_general(row_hot, ones.astype(BF16), contract, preferred_element_type=F32)
    )
    for step in range(2):
        spread = jnp.where(lane_hot, observed_ref[step], 0.0)
        total = None
        for part in split3(spread):
            t = lax.dot_general(row_hot, part, contract, preferred_element_type=F32)
            total = t if total is None else total + t
        put_counts(1 + step, total)
    sources = [(prev_out, 0), (next_out, 0), (scale_out, 0)]
    sources += [(counts_out, 0), (counts_out, 64), (counts_out, 128)]
    for which, (field, base) in enumerate(sources):
        for k, v in enumerate(pack_low(sh, [field[base + qr] for qr in range(16)])):
            message[8 * which + k] = v


def without_far(sh, field):
    def get(p, qr):
        if p < 4:
            return field[p * 16 + qr]
        return jnp.where(sh.low, half_turn(field[qr]), 0.0)

    return get


def force_kernel(u_ref, lam_ref, stiff, u_force, lam_force, blocks, scratch):
    sh = Shifts()
    for field, out in ((u_ref, u_force), (lam_ref, lam_force)):
        expand(sh, without_far(sh, field), blocks)
        force(sh, blocks, stiff, scratch, out)


def far_plane_kernel(
    slab_ref, message, stiff, u_in, lam_in, u_force, lam_force, far, near, column
):
    sh = Shifts()
    odd = is_odd(slab_ref)
    for n in range(25):
        f = backward_line([float(DERIVATIVE[k, 4]) * stiff[k * 25 + n] for k in range(5)])
        for k in range(5):
            column[k * 25 + n] = f[k]
    for which, (source, out) in enumerate(((u_in, u_force), (lam_in, lam_force))):
        face = [None] * 25
        for q in range(4):
            for r in range(4):
                v = jnp.where(sh.low, 0.0, to_high(message, 8 * which, q * 4 + r))
                face[q * 5 + r] = v
                if r == 0:
                    face[q * 5 + 4] = sh.next_z(v)
                if q == 0:
                    face[20 + r] = sh.next_y(v)
                    if r == 0:
                        face[24] = sh.next_z(face[20])
        for p in range(5):
            added = [column[p * 25 + n] * face[n] for n in range(25)]
            if p == 4:
                for a in range(5):
                    for at in ([a * 5 + k for k in range(5)], [k * 5 + a for k in range(5)]):
                        g = forward_line([face[n] for n in at])
                        f = backward_line([stiff[100 + n] * g[k] for k, n in enumerate(at)])
                        for k, n in enumerate(at):
                            added[n] = added[n] + f[k]
            for qr, v in enumerate(assemble(sh, added)):
                out[p * 16 + qr] = source[p * 16 + qr] + v
        put_messages(sh, odd, out, far, near, 8 * which)


def step_one_kernel(
    slab_ref,
    u_ref,
    lam_ref,
    prev_ref,
    next_ref,
    scale_ref,
    stiff,
    message0,
    message1,
    u_force,
    lam_force,
    far_in,
    near_in,
    u1_out,
    lam1_out,
    scale_out,
    u1_force,
    far,
    near,
    blocks,
    scratch,
):
    sh = Shifts()
    odd = is_odd(slab_ref)
    incoming = Incoming(odd, far_in, near_in)
    u0, lam2 = extended(sh, u_ref, message0, 0), extended(sh, lam_ref, message0, 8)
    before, after = extended(sh, prev_ref, message1, 0), extended(sh, next_ref, message1, 8)
    scale = extended(sh, scale_ref, message1, 16)
    u_total = assembled(sh, u_force, incoming, 0)
    lam_total = assembled(sh, lam_force, incoming, 8)
    for p in range(5):
        for qr in range(16):
            s = scale(p, qr)
            scale_out[p * 16 + qr] = s
            u1_out[p * 16 + qr] = 2.0 * u0(p, qr) - before(p, qr) - s * u_total(p, qr)
            lam1_out[p * 16 + qr] = 2.0 * lam2(p, qr) - after(p, qr) - s * lam_total(p, qr)
    expand(sh, stored(u1_out), blocks)
    force(sh, blocks, stiff, scratch, u1_force)
    put_messages(sh, odd, u1_force, far, near, 0)


def mean_square(energy):
    total = jnp.sum(energy, axis=1, keepdims=True)
    return total / SAMPLES + EPSILON


def step_two_kernel(
    slab_ref,
    energy_ref,
    u_ref,
    message0,
    message1,
    u1_ref,
    lam1_ref,
    scale,
    counts,
    stiff,
    u1_force,
    far_in,
    near_in,
    u2_out,
    lam1_out,
    source_out,
    u2_force,
    lam1_force,
    far,
    near,
    blocks,
    scratch,
):
    sh = Shifts()
    odd = is_odd(slab_ref)
    incoming = Incoming(odd, far_in, near_in)
    inverse = jnp.broadcast_to(1.0 / mean_square(energy_ref[...]), (8, 128))
    u0 = extended(sh, u_ref, message0, 0)
    count = extended(sh, counts.at[pl.ds(0, 64)], message1, 24)
    seen = [extended(sh, counts.at[pl.ds(64 + 64 * n, 64)], message1, 32 + 8 * n) for n in range(2)]
    total = assembled(sh, u1_force, incoming, 0)
    for p in range(5):
        for qr in range(16):
            at = p * 16 + qr
            s, u1, c = scale[at], u1_ref[at], count(p, qr)
            u2 = 2.0 * u1 - u0(p, qr) - s * total(p, qr)
            u2_out[at] = u2
            lam1_out[at] = lam1_ref[at] + s * ((c * u2 - seen[1](p, qr)) * inverse)
            source_out[at] = s * ((c * u1 - seen[0](p, qr)) * inverse)
    expand(sh, stored(lam1_out), blocks)
    force(sh, blocks, stiff, scratch, lam1_force)
    put_messages(sh, odd, lam1_force, far, near, 0)
    expand(sh, stored(u2_out), blocks)
    force(sh, blocks, stiff, scratch, u2_force)
    put_messages(sh, odd, u2_force, far, near, 8)


def middle_kernel(u1_ref, lam1_ref, u2_ref, lam_ref, message0, acc, first, second):
    sh = Shifts()
    expand(sh, stored(u1_ref), first)
    expand(sh, stored(lam1_ref), second)
    products(first, second, acc, True)
    expand(sh, stored(u2_ref), first)
    expand(sh, extended(sh, lam_ref, message0, 8), second)
    products(first, second, acc, False)


def last_kernel(
    slab_ref,
    event_ref,
    u_ref,
    lam_ref,
    message0,
    lam1_ref,
    scale,
    source,
    lam1_force,
    far_in,
    near_in,
    acc_ref,
    out0,
    out1,
    out2,
    out3,
    lam0,
    first,
    second,
    acc,
    flat,
):
    sh = Shifts()
    lam2 = extended(sh, lam_ref, message0, 8)
    total = assembled(sh, lam1_force, Incoming(is_odd(slab_ref), far_in, near_in), 0)
    for p in range(5):
        for qr in range(16):
            at = p * 16 + qr
            lam0[at] = (
                2.0 * lam1_ref[at] - lam2(p, qr) - scale[at] * total(p, qr) + source[at]
            )
    expand(sh, extended(sh, u_ref, message0, 0), first)
    expand(sh, stored(lam0), second)
    for i in range(125):
        acc[i] = acc_ref[i]
    products(first, second, acc, False)
    for p in range(5):
        for q in range(5):
            for r in range(5):
                at = p * 25 + q * 5 + r
                weight = float(-WEIGHTS[p] * WEIGHTS[q] * WEIGHTS[r])
                v = weight * acc[at]
                for i in range(2):
                    row = 4 * ((2 * p + i) * 25 + q * 5 + r)
                    flat[row : row + 4, :] = v[4 * i : 4 * i + 4]
    event = event_ref[0]
    for k, out in enumerate((out0, out1, out2, out3)):
        out[...] = flat[pl.ds(jnp.bitwise_xor(event, k), 250, stride=4), :]


def misfit_kernel(
    slab_ref,
    receivers_ref,
    observed_ref,
    u1_ref,
    u2_ref,
    scale,
    u2_force,
    far_in,
    near_in,
    out,
    u3,
):
    sh = Shifts()
    total = assembled(sh, u2_force, Incoming(is_odd(slab_ref), far_in, near_in), 8)
    for p in range(4):
        for qr in range(16):
            at = p * 16 + qr
            u3[at] = 2.0 * u2_ref[at] - u1_ref[at] - scale[at] * total(p, qr)
    row_hot, lane_hot = one_hots(receivers_ref[...])
    row_hot = jnp.where(row_hot, 1.0, 0.0).astype(BF16)
    squares = jnp.zeros((1, 128), F32)
    for step, field in enumerate((u1_ref, u2_ref, u3)):
        values = field[pl.ds(0, 64)].reshape(512, 128)
        picked = None
        for part in split3(values):
            t = lax.dot_general(
                part, row_hot, (((0,), (0,)), ((), ())), preferred_element_type=F32
            )
            picked = t if picked is None else picked + t
        syn = jnp.sum(jnp.where(lane_hot, picked, 0.0), axis=0, keepdims=True)
        residual = syn - observed_ref[step]
        squares = squares + residual * residual
    out[...] = jnp.broadcast_to(jnp.sum(squares, axis=1, keepdims=True), (1, 128))


def sum_kernel(a, b, c, d, misfit, total_out, message):
    total = a[...] + b[...] + c[...] + d[...]
    total_out[...] = total
    largest = jnp.max(jnp.max(jnp.abs(total), axis=0, keepdims=True), axis=1, keepdims=True)
    first_half = lax.broadcasted_iota(jnp.int32, (1, 128), 1) < 64
    message[...] = jnp.where(first_half, jnp.broadcast_to(largest, (1, 128)), misfit[...])


def divide_kernel(event_ref, total, gathered, energy_ref, out, misfit_out):
    rows = gathered[...]
    first_half = lax.broadcasted_iota(jnp.int32, (1, 128), 1) < 64
    top = jnp.where(first_half, jnp.max(rows, axis=0, keepdims=True), 0.0)
    largest = jnp.max(top, axis=1, keepdims=True)
    spaces = gathered.shape[0] // 4
    mine = gathered[pl.ds(pl.multiple_of(event_ref[0] * spaces, spaces), spaces), :]
    squares = jnp.where(first_half, 0.0, jnp.sum(mine, axis=0, keepdims=True))
    squares = jnp.max(squares, axis=1, keepdims=True)
    misfit_out[...] = jnp.broadcast_to(
        0.5 * squares / (SAMPLES * mean_square(energy_ref[...])), (1, 128)
    )
    out[...] = (total[...] / (largest + EPSILON)).reshape(250, 1, 128)


COST = 16 << 20
VMEM_GRANT = 16 << 20
VMEM_SPEC = pl.BlockSpec(memory_space=pltpu.VMEM)
HBM_SPEC = pl.BlockSpec(memory_space=pltpu.MemorySpace.HBM)
SMEM_SPEC = pl.BlockSpec(memory_space=pltpu.SMEM)


def call(kernel, args, outs, scratch=(), scalars=0, loads=0):
    buffers = [pltpu.VMEM(arg.shape, F32) for arg in args[scalars : scalars + loads]]
    semaphores = [pltpu.SemaphoreType.DMA((loads,))] if loads else []
    return pl.pallas_call(
        kernel,
        out_shape=[jax.ShapeDtypeStruct(shape, F32) for shape in outs],
        in_specs=[SMEM_SPEC] * scalars
        + [HBM_SPEC] * loads
        + [VMEM_SPEC] * (len(args) - scalars - loads),
        out_specs=[VMEM_SPEC] * len(outs),
        scratch_shapes=[pltpu.VMEM(shape, F32) for shape in scratch] + buffers + semaphores,
        cost_estimate=pl.CostEstimate(flops=0, bytes_accessed=COST, transcendentals=0),
        compiler_params=pltpu.CompilerParams(vmem_limit_bytes=VMEM_GRANT),
    )(*args)


def vectors(count):
    return (count, 8, 128)


def to_left(array):
    devices = lax.axis_size("space")
    return lax.ppermute(array, "space", [(i, i - 1) for i in range(1, devices)])


def exchange(far, near):
    devices = lax.axis_size("space")
    far_pairs = [(i, i + 1 if i % 2 else i - 1) for i in range(1, devices - 1)]
    near_pairs = [(i, i - 1 if i % 2 else i + 1) for i in range(devices)]
    return (lax.ppermute(far, "space", far_pairs), lax.ppermute(near, "space", near_pairs))


def across(array, stride):
    devices = lax.axis_size("space")
    return array + lax.ppermute(array, "space", [(i, i ^ stride) for i in range(devices)])


def shards(state_now, state_prev, adjoint_now, adjoint_next, modulus, density, receivers, observed):
    slab = lax.axis_index("space").astype(jnp.int32).reshape(1)
    event = lax.axis_index("event").astype(jnp.int32).reshape(1)
    receivers = receivers.reshape(1, 128)
    observed = jnp.transpose(observed, (1, 0, 2))
    modulus = jnp.transpose(modulus, (0, 1, 2, 4, 3, 5))

    energy = jnp.sum(observed * observed, axis=0)
    energy = across(energy, 1)

    u0, lam2, planes = call(
        first_kernel,
        (state_now[0], adjoint_now[0]),
        [vectors(64), vectors(64), vectors(16)],
        [(4, 128, 128)],
        loads=2,
    )
    energy = across(energy, 16)
    message0 = to_left(planes)
    before, after, scale, stiff, counts, planes = call(
        second_kernel,
        (slab, state_prev[0], adjoint_next[0], density, modulus, receivers, observed),
        [vectors(64), vectors(64), vectors(64), vectors(125), vectors(192), vectors(48)],
        [(4, 128, 128)],
        scalars=1,
        loads=4,
    )
    energy = across(energy, 2)
    message1 = to_left(planes)
    u_force, lam_force = call(
        force_kernel,
        (u0, lam2, stiff),
        [vectors(80), vectors(80)],
        [vectors(125), vectors(125)],
    )
    energy = across(energy, 32)
    u_force, lam_force, far, near = call(
        far_plane_kernel,
        (slab, message0, stiff, u_force, lam_force),
        [vectors(80), vectors(80), vectors(16), vectors(16)],
        [vectors(125)],
        scalars=1,
    )
    energy = across(energy, 4)
    far, near = exchange(far, near)
    u1, lam1, scale, u1_force, far, near = call(
        step_one_kernel,
        (
            slab,
            u0,
            lam2,
            before,
            after,
            scale,
            stiff,
            message0,
            message1,
            u_force,
            lam_force,
            far,
            near,
        ),
        [vectors(80)] * 4 + [vectors(8)] * 2,
        [vectors(125), vectors(125)],
        scalars=1,
    )
    energy = across(energy, 8)
    far, near = exchange(far, near)
    u2, lam1, source, u2_force, lam1_force, far, near = call(
        step_two_kernel,
        (
            slab,
            energy,
            u0,
            message0,
            message1,
            u1,
            lam1,
            scale,
            counts,
            stiff,
            u1_force,
            far,
            near,
        ),
        [vectors(80)] * 5 + [vectors(16)] * 2,
        [vectors(125), vectors(125)],
        scalars=1,
    )
    far, near = exchange(far, near)
    (acc,) = call(
        middle_kernel,
        (u1, lam1, u2, lam2, message0),
        [vectors(125)],
        [vectors(125), vectors(125)],
    )
    pieces = call(
        last_kernel,
        (slab, event, u0, lam2, message0, lam1, scale, source, lam1_force, far, near, acc),
        [(250, 128)] * 4,
        [vectors(80), vectors(125), vectors(125), vectors(125), (1000, 128)],
        scalars=2,
    )
    events = lax.axis_size("event")
    others = [
        lax.ppermute(pieces[k], "event", [(i, i ^ k) for i in range(events)])
        for k in (1, 2, 3)
    ]
    (squares,) = call(
        misfit_kernel,
        (slab, receivers, observed, u1, u2, scale, u2_force, far, near),
        [(1, 128)],
        [vectors(64)],
        scalars=1,
    )
    total, message = call(
        sum_kernel, (pieces[0], *others, squares), [(250, 128), (1, 128)]
    )
    everyone = ("event", "space")
    devices = lax.axis_size("event") * lax.axis_size("space")
    gathered = lax.all_to_all(
        jnp.broadcast_to(message[None], (devices, 1, 128)), everyone, 0, 0
    )
    kernel, misfit = call(
        divide_kernel,
        (event, total, gathered.reshape(devices, 128), energy),
        [(250, 1, 128), (1, 128)],
        scalars=1,
    )
    kernel = jnp.transpose(kernel.reshape(5, 2, 5, 5, 1, 128), (0, 1, 2, 4, 3, 5))
    return (kernel, misfit[0, :1])


def solution(mesh):
    in_specs = (
        P("event", "space", None, None),
        P("event", "space", None, None),
        P("event", "space", None, None),
        P("event", "space", None, None),
        P(None, "space", None, None, None, None),
        P("space", None, None),
        P("space"),
        P("event", None, "space"),
    )
    out_specs = (P(None, "space", None, "event", None, None), P("event"))

    return jax.shard_map(shards, mesh=mesh, in_specs=in_specs, out_specs=out_specs, check_vma=False)
```

profile of v0, /device:TPU:1, one launch (start us, length us, event | category | flops | bytes accessed | tf_op | source)
XLA Modules:
  0.0 121.0 jit_solution(9847456038125778862)
XLA Ops:
  0.6 0.0 copy-start.6
  0.6 0.0 copy-start.7
  0.7 0.7 copy-done.6
  1.3 0.0 copy-done.7
  1.3 0.0 copy-start
  1.3 1.0 copy-done
  2.4 0.0 copy-start.3
  2.4 0.9 copy-done.3
  3.3 0.0 copy-start.4
  3.3 0.9 copy-done.4
  4.3 0.0 copy-start.5
  4.3 0.9 copy-done.5
  5.2 0.0 copy-start.1
  5.2 0.0 copy-start.2
  5.2 2.2 %shard_map.96 = (f32[64,8,128]{2,1,0:T(8,128)S(1)}, f32[64,8,128]{2,1,0:T(8,128)S(1)}, f32[64,8,128]{2,1,0:T(8,128)S(1)}, f32[125,8,128]{2,1,0:T(8,128)S(1)}, f3...) custom-call(s32[1]{0:T(128)} %bitcast.1.slab_ref, f32[8,16,512]{2,1,0:T(8,128)S(1)} %bitcast.21, ...), custom_call_target="tpu_custom_call" | custom-call | bytes 16777216 | tf_op jit(solution)/shard_map/pallas_call | solution.py:686
  7.4 1.3 %collective-permute-start.7 = (f32[48,8,128]{2,1,0:T(8,128)S(1)}, f32[48,8,128]{2,1,0:T(8,128)S(1)}, u32[]{:S(2)}, u32[]{:S(2)}) collective-permute-start(f32[48,8,128]{2,1,0:T(8,128)S(1)} %get-tuple-element.41), channel_id=1, source_target_pairs={{1,0},{2,1},{3,2},{4,3},{5,4},{6,5},{7,6},{8,7},{9,8},{10,9},{11,1... | collective-permute-start | bytes 589832 | tf_op jit(solution)/shard_map/ppermute | solution.py:705
  8.7 0.0 copy-done.1
  8.7 0.0 copy-done.2
  8.7 0.9 shard_map.95
  9.6 1.3 %collective-permute-start = (f32[16,8,128]{2,1,0:T(8,128)S(1)}, f32[16,8,128]{2,1,0:T(8,128)S(1)}, u32[]{:S(2)}, u32[]{:S(2)}) collective-permute-start(f32[16,8,128]{2,1,0:T(8,128)S(1)} %get-tuple-element.40), channel_id=1, source_target_pairs={{1,0},{2,1},{3,2},{4,3},{5,4},{6,5},{7,6},{8,7},{9,8},{10,9},{11,1... | collective-permute-start | bytes 196616 | tf_op jit(solution)/shard_map/ppermute | solution.py:705
  10.9 1.4 %shard_map.97 = (f32[80,8,128]{2,1,0:T(8,128)S(1)}, f32[80,8,128]{2,1,0:T(8,128)S(1)}) custom-call(f32[64,8,128]{2,1,0:T(8,128)S(1)} %get-tuple-element.38.u_ref, f32[64,8,128]{2,1,0:T(8,128)S(1)} %get-tuple-element.39.lam_ref, f32[125,8,128]{2,1,0:T(8,128)S(1)} %get-tuple-element.45.stiff), custom_call_target="tpu_custom_call" | custom-call | bytes 16777216 | tf_op jit(solution)/shard_map/pallas_call | solution.py:686
  12.3 4.4 %collective-permute-done.message.message0 = f32[16,8,128]{2,1,0:T(8,128)S(1)} collective-permute-done((f32[16,8,128]{2,1,0:T(8,128)S(1)}, f32[16,8,128]{2,1,0:T(8,128)S(1)}, u32[]{:S(2)}, u32[]{:S(2)}) %collective-permute-start) | collective-permute-done | bytes 65568 | tf_op jit(solution)/shard_map/ppermute | solution.py:705
  16.7 0.4 shard_map.98
  17.1 0.7 collective-permute-start.8
  17.8 4.5 %collective-permute-start.9 = (f32[16,8,128]{2,1,0:T(8,128)S(1)}, f32[16,8,128]{2,1,0:T(8,128)S(1)}, u32[]{:S(2)}, u32[]{:S(2)}) collective-permute-start(f32[16,8,128]{2,1,0:T(8,128)S(1)} %get-tuple-element.51), channel_id=1, source_target_pairs={{0,1},{1,0},{2,3},{3,2},{4,5},{5,4},{6,7},{7,6},{8,9},{9,8},{10,11... | collective-permute-start | bytes 196616 | tf_op jit(solution)/shard_map/ppermute | solution.py:712
  22.3 0.1 collective-permute-start.1
  22.4 0.0 collective-permute-done.8.far_in
  22.4 1.5 %collective-permute-done.9.near_in = f32[16,8,128]{2,1,0:T(8,128)S(1)} collective-permute-done((f32[16,8,128]{2,1,0:T(8,128)S(1)}, f32[16,8,128]{2,1,0:T(8,128)S(1)}, u32[]{:S(2)}, u32[]{:S(2)}) %collective-permute-start.9) | collective-permute-done | bytes 65568 | tf_op jit(solution)/shard_map/ppermute | solution.py:712
  24.0 0.0 collective-permute-done.7.message1
  24.0 0.9 shard_map.99
  24.9 0.7 collective-permute-start.10
  25.6 11.0 %collective-permute-start.11 = (f32[8,8,128]{2,1,0:T(8,128)S(1)}, f32[8,8,128]{2,1,0:T(8,128)S(1)}, u32[]{:S(2)}, u32[]{:S(2)}) collective-permute-start(f32[8,8,128]{2,1,0:T(8,128)S(1)} %get-tuple-element.58), channel_id=1, source_target_pairs={{0,1},{1,0},{2,3},{3,2},{4,5},{5,4},{6,7},{7,6},{8,9},{9,8},{10,11... | collective-permute-start | bytes 98312 | tf_op jit(solution)/shard_map/ppermute | solution.py:712
  36.6 0.0 collective-permute-done.1
  36.6 15.9 %collective-permute-start.2 = (f32[1,128]{1,0:T(1,128)S(1)}, f32[1,128]{1,0:T(1,128)S(1)}, u32[]{:S(2)}, u32[]{:S(2)}) collective-permute-start(f32[1,128]{1,0:T(1,128)S(1)} %bitcast_add_fusion), channel_id=1, source_target_pairs={{0,16},{1,17},{2,18},{3,19},{4,20},{5,21},{6,22},{7,23},{8,24},{9,... | collective-permute-start | bytes 1544 | tf_op jit(solution)/shard_map/ppermute | solution.py:717
  52.5 1.0 collective-permute-done.2
  53.5 0.0 collective-permute-start.3
  53.5 3.9 %collective-permute-done.3 = f32[1,128]{1,0:T(1,128)S(1)} collective-permute-done((f32[1,128]{1,0:T(1,128)S(1)}, f32[1,128]{1,0:T(1,128)S(1)}, u32[]{:S(2)}, u32[]{:S(2)}) %collective-permute-start.3) | collective-permute-done | bytes 544 | tf_op jit(solution)/shard_map/ppermute | solution.py:717
  57.4 3.3 %collective-permute-start.4 = (f32[1,128]{1,0:T(1,128)S(1)}, f32[1,128]{1,0:T(1,128)S(1)}, u32[]{:S(2)}, u32[]{:S(2)}) collective-permute-start(f32[1,128]{1,0:T(1,128)S(1)} %add.20), channel_id=1, source_target_pairs={{0,32},{1,33},{2,34},{3,35},{4,36},{5,37},{6,38},{7,39},{8,40},{9,... | collective-permute-start | bytes 1544 | tf_op jit(solution)/shard_map/ppermute | solution.py:717
  60.7 1.0 collective-permute-done.4
  61.7 0.0 collective-permute-start.5
  61.7 3.3 %collective-permute-done.5 = f32[1,128]{1,0:T(1,128)S(1)} collective-permute-done((f32[1,128]{1,0:T(1,128)S(1)}, f32[1,128]{1,0:T(1,128)S(1)}, u32[]{:S(2)}, u32[]{:S(2)}) %collective-permute-start.5) | collective-permute-done | bytes 544 | tf_op jit(solution)/shard_map/ppermute | solution.py:717
  65.0 0.0 collective-permute-start.6
  65.0 6.3 %collective-permute-done.6 = f32[1,128]{1,0:T(1,128)S(1)} collective-permute-done((f32[1,128]{1,0:T(1,128)S(1)}, f32[1,128]{1,0:T(1,128)S(1)}, u32[]{:S(2)}, u32[]{:S(2)}) %collective-permute-start.6) | collective-permute-done | bytes 544 | tf_op jit(solution)/shard_map/ppermute | solution.py:717
  71.3 0.0 collective-permute-done.10.far_in
  71.3 0.0 collective-permute-done.11.near_in
  71.3 1.6 %shard_map.100 = (f32[80,8,128]{2,1,0:T(8,128)S(1)}, f32[80,8,128]{2,1,0:T(8,128)S(1)}, f32[80,8,128]{2,1,0:T(8,128)S(1)}, f32[80,8,128]{2,1,0:T(8,128)S(1)}, f3...) custom-call(s32[1]{0:T(128)} %bitcast.1.slab_ref, f32[1,128]{1,0:T(1,128)S(1)} %add.23.energy_ref, ...), custom_call_target="tpu_custom_call" | custom-call | bytes 16777216 | tf_op jit(solution)/shard_map/pallas_call | solution.py:686
  72.9 0.7 collective-permute-start.12
  73.6 2.6 %collective-permute-start.13 = (f32[16,8,128]{2,1,0:T(8,128)S(1)}, f32[16,8,128]{2,1,0:T(8,128)S(1)}, u32[]{:S(2)}, u32[]{:S(2)}) collective-permute-start(f32[16,8,128]{2,1,0:T(8,128)S(1)} %get-tuple-element.63), channel_id=1, source_target_pairs={{0,1},{1,0},{2,3},{3,2},{4,5},{5,4},{6,7},{7,6},{8,9},{9,8},{10,11... | collective-permute-start | bytes 196616 | tf_op jit(solution)/shard_map/ppermute | solution.py:712
  76.2 1.4 %shard_map.101.acc_ref = f32[125,8,128]{2,1,0:T(8,128)S(1)} custom-call(f32[80,8,128]{2,1,0:T(8,128)S(1)} %get-tuple-element.52.u1_ref, f32[80,8,128]{2,1,0:T(8,128)S(1)} %get-tuple-element.59.lam1_ref, f32[80,8,128]{2,1,0:T(8,128)S(1)} %get-tuple-element.64.u2_ref, f32[64,8,128]{2,1,0:T(8,128)S(1)} %get-tuple-element.39.lam_ref, ...), custom_call_target="tpu_custom_call" | custom-call | bytes 16777216 | tf_op jit(solution)/shard_map/pallas_call | solution.py:686
  77.6 0.0 collective-permute-done.12.far_in
  77.6 0.3 collective-permute-done.13.near_in
  77.9 0.9 shard_map.102
  78.8 8.5 %collective-permute-start.14 = (f32[250,128]{1,0:T(8,128)S(1)}, f32[250,128]{1,0:T(8,128)S(1)}, u32[]{:S(2)}, u32[]{:S(2)}) collective-permute-start(f32[250,128]{1,0:T(8,128)S(1)} %get-tuple-element.66), channel_id=1, source_target_pairs={{0,64},{64,0},{128,192},{192,128},{1,65},{65,1},{129,193},{193,129... | collective-permute-start | bytes 384008 | tf_op jit(solution)/shard_map/ppermute | solution.py:825
  87.2 0.0 collective-permute-start.15
  87.2 1.7 %collective-permute-start.16 = (f32[250,128]{1,0:T(8,128)S(1)}, f32[250,128]{1,0:T(8,128)S(1)}, u32[]{:S(2)}, u32[]{:S(2)}) collective-permute-start(f32[250,128]{1,0:T(8,128)S(1)} %get-tuple-element.68), channel_id=1, source_target_pairs={{0,192},{64,128},{128,64},{192,0},{1,193},{65,129},{129,65},{193,1... | collective-permute-start | bytes 384008 | tf_op jit(solution)/shard_map/ppermute | solution.py:825
  88.9 0.6 shard_map.103.misfit
  89.6 0.0 collective-permute-done.14.b
  89.6 2.6 %collective-permute-done.15.c = f32[250,128]{1,0:T(8,128)S(1)} collective-permute-done((f32[250,128]{1,0:T(8,128)S(1)}, f32[250,128]{1,0:T(8,128)S(1)}, u32[]{:S(2)}, u32[]{:S(2)}) %collective-permute-start.15) | collective-permute-done | bytes 128032 | tf_op jit(solution)/shard_map/ppermute | solution.py:825
  92.2 3.1 %collective-permute-done.16.d = f32[250,128]{1,0:T(8,128)S(1)} collective-permute-done((f32[250,128]{1,0:T(8,128)S(1)}, f32[250,128]{1,0:T(8,128)S(1)}, u32[]{:S(2)}, u32[]{:S(2)}) %collective-permute-start.16) | collective-permute-done | bytes 128032 | tf_op jit(solution)/shard_map/ppermute | solution.py:825
  95.2 0.1 shard_map.104
  95.4 0.1 broadcast_in_dim.9
  95.4 24.8 %all_to_all.5 = f32[256,1,128]{2,1,0:T(1,128)S(1)} all-to-all(f32[256,1,128]{2,1,0:T(1,128)S(1)} %broadcast_in_dim.9), channel_id=1, replica_groups=mesh['event'=4,'space'=64] {'event','space'}, dimensions={0} | all-to-all | bytes 262144 | tf_op jit(solution)/shard_map/all_to_all | solution.py:840
  120.2 0.8 shard_map.105
  (7 shorter events, 0.0 us)
Async XLA Ops:
  0.6 0.7 copy-start.6
  0.6 0.7 copy-start.7
  1.3 1.0 copy-start
  2.4 0.9 copy-start.3
  3.3 0.9 copy-start.4
  4.3 0.9 copy-start.5
  5.2 3.5 %copy-start.1 = (f32[1,8,16,512]{3,2,1,0:T(8,128)S(1)}, f32[1,8,16,512]{3,2,1,0:T(8,128)}, u32[]{:S(2)}) copy-start(f32[1,8,16,512]{3,2,1,0:T(8,128)} %param.8) | copy-start | bytes 786436
  5.2 3.5 %copy-start.2 = (f32[1,8,16,512]{3,2,1,0:T(8,128)S(1)}, f32[1,8,16,512]{3,2,1,0:T(8,128)}, u32[]{:S(2)}) copy-start(f32[1,8,16,512]{3,2,1,0:T(8,128)} %param.10) | copy-start | bytes 786436
  7.4 16.6 %collective-permute-start.7 = (f32[48,8,128]{2,1,0:T(8,128)S(1)}, f32[48,8,128]{2,1,0:T(8,128)S(1)}, u32[]{:S(2)}, u32[]{:S(2)}) collective-permute-start(f32[48,8,128]{2,1,0:T(8,128)S(1)} %get-tuple-element.41), channel_id=1, source_target_pairs={{1,0},{2,1},{3,2},{4,3},{5,4},{6,5},{7,6},{8,7},{9,8},{10,9},{11,1... | collective-permute-start | bytes 589832 | tf_op jit(solution)/shard_map/ppermute | solution.py:705
  9.6 7.1 %collective-permute-start = (f32[16,8,128]{2,1,0:T(8,128)S(1)}, f32[16,8,128]{2,1,0:T(8,128)S(1)}, u32[]{:S(2)}, u32[]{:S(2)}) collective-permute-start(f32[16,8,128]{2,1,0:T(8,128)S(1)} %get-tuple-element.40), channel_id=1, source_target_pairs={{1,0},{2,1},{3,2},{4,3},{5,4},{6,5},{7,6},{8,7},{9,8},{10,9},{11,1... | collective-permute-start | bytes 196616 | tf_op jit(solution)/shard_map/ppermute | solution.py:705
  17.1 5.3 %collective-permute-start.8 = (f32[16,8,128]{2,1,0:T(8,128)S(1)}, f32[16,8,128]{2,1,0:T(8,128)S(1)}, u32[]{:S(2)}, u32[]{:S(2)}) collective-permute-start(f32[16,8,128]{2,1,0:T(8,128)S(1)} %get-tuple-element.50), channel_id=1, source_target_pairs={{1,2},{2,1},{3,4},{4,3},{5,6},{6,5},{7,8},{8,7},{9,10},{10,9},{11,... | collective-permute-start | bytes 196616 | tf_op jit(solution)/shard_map/ppermute | solution.py:712
  17.8 6.2 %collective-permute-start.9 = (f32[16,8,128]{2,1,0:T(8,128)S(1)}, f32[16,8,128]{2,1,0:T(8,128)S(1)}, u32[]{:S(2)}, u32[]{:S(2)}) collective-permute-start(f32[16,8,128]{2,1,0:T(8,128)S(1)} %get-tuple-element.51), channel_id=1, source_target_pairs={{0,1},{1,0},{2,3},{3,2},{4,5},{5,4},{6,7},{7,6},{8,9},{9,8},{10,11... | collective-permute-start | bytes 196616 | tf_op jit(solution)/shard_map/ppermute | solution.py:712
  22.3 14.2 %collective-permute-start.1 = (f32[1,128]{1,0:T(1,128)S(1)}, f32[1,128]{1,0:T(1,128)S(1)}, u32[]{:S(2)}, u32[]{:S(2)}) collective-permute-start(f32[1,128]{1,0:T(1,128)S(1)} %bitcast.28), channel_id=1, source_target_pairs={{0,1},{1,0},{2,3},{3,2},{4,5},{5,4},{6,7},{7,6},{8,9},{9,8},{10,11... | collective-permute-start | bytes 1544 | tf_op jit(solution)/shard_map/ppermute | solution.py:717
  24.9 46.4 %collective-permute-start.10 = (f32[8,8,128]{2,1,0:T(8,128)S(1)}, f32[8,8,128]{2,1,0:T(8,128)S(1)}, u32[]{:S(2)}, u32[]{:S(2)}) collective-permute-start(f32[8,8,128]{2,1,0:T(8,128)S(1)} %get-tuple-element.57), channel_id=1, source_target_pairs={{1,2},{2,1},{3,4},{4,3},{5,6},{6,5},{7,8},{8,7},{9,10},{10,9},{11,... | collective-permute-start | bytes 98312 | tf_op jit(solution)/shard_map/ppermute | solution.py:712
  25.6 45.7 %collective-permute-start.11 = (f32[8,8,128]{2,1,0:T(8,128)S(1)}, f32[8,8,128]{2,1,0:T(8,128)S(1)}, u32[]{:S(2)}, u32[]{:S(2)}) collective-permute-start(f32[8,8,128]{2,1,0:T(8,128)S(1)} %get-tuple-element.58), channel_id=1, source_target_pairs={{0,1},{1,0},{2,3},{3,2},{4,5},{5,4},{6,7},{7,6},{8,9},{9,8},{10,11... | collective-permute-start | bytes 98312 | tf_op jit(solution)/shard_map/ppermute | solution.py:712
  36.6 16.9 %collective-permute-start.2 = (f32[1,128]{1,0:T(1,128)S(1)}, f32[1,128]{1,0:T(1,128)S(1)}, u32[]{:S(2)}, u32[]{:S(2)}) collective-permute-start(f32[1,128]{1,0:T(1,128)S(1)} %bitcast_add_fusion), channel_id=1, source_target_pairs={{0,16},{1,17},{2,18},{3,19},{4,20},{5,21},{6,22},{7,23},{8,24},{9,... | collective-permute-start | bytes 1544 | tf_op jit(solution)/shard_map/ppermute | solution.py:717
  53.5 3.9 %collective-permute-start.3 = (f32[1,128]{1,0:T(1,128)S(1)}, f32[1,128]{1,0:T(1,128)S(1)}, u32[]{:S(2)}, u32[]{:S(2)}) collective-permute-start(f32[1,128]{1,0:T(1,128)S(1)} %add.19), channel_id=1, source_target_pairs={{0,2},{1,3},{2,0},{3,1},{4,6},{5,7},{6,4},{7,5},{8,10},{9,11},{10,... | collective-permute-start | bytes 1544 | tf_op jit(solution)/shard_map/ppermute | solution.py:717
  57.4 4.2 %collective-permute-start.4 = (f32[1,128]{1,0:T(1,128)S(1)}, f32[1,128]{1,0:T(1,128)S(1)}, u32[]{:S(2)}, u32[]{:S(2)}) collective-permute-start(f32[1,128]{1,0:T(1,128)S(1)} %add.20), channel_id=1, source_target_pairs={{0,32},{1,33},{2,34},{3,35},{4,36},{5,37},{6,38},{7,39},{8,40},{9,... | collective-permute-start | bytes 1544 | tf_op jit(solution)/shard_map/ppermute | solution.py:717
  61.7 3.3 %collective-permute-start.5 = (f32[1,128]{1,0:T(1,128)S(1)}, f32[1,128]{1,0:T(1,128)S(1)}, u32[]{:S(2)}, u32[]{:S(2)}) collective-permute-start(f32[1,128]{1,0:T(1,128)S(1)} %add.21), channel_id=1, source_target_pairs={{0,4},{1,5},{2,6},{3,7},{4,0},{5,1},{6,2},{7,3},{8,12},{9,13},{10,... | collective-permute-start | bytes 1544 | tf_op jit(solution)/shard_map/ppermute | solution.py:717
  65.0 6.3 %collective-permute-start.6 = (f32[1,128]{1,0:T(1,128)S(1)}, f32[1,128]{1,0:T(1,128)S(1)}, u32[]{:S(2)}, u32[]{:S(2)}) collective-permute-start(f32[1,128]{1,0:T(1,128)S(1)} %add.22), channel_id=1, source_target_pairs={{0,8},{1,9},{2,10},{3,11},{4,12},{5,13},{6,14},{7,15},{8,0},{9,1},... | collective-permute-start | bytes 1544 | tf_op jit(solution)/shard_map/ppermute | solution.py:717
  72.9 4.6 %collective-permute-start.12 = (f32[16,8,128]{2,1,0:T(8,128)S(1)}, f32[16,8,128]{2,1,0:T(8,128)S(1)}, u32[]{:S(2)}, u32[]{:S(2)}) collective-permute-start(f32[16,8,128]{2,1,0:T(8,128)S(1)} %get-tuple-element.62), channel_id=1, source_target_pairs={{1,2},{2,1},{3,4},{4,3},{5,6},{6,5},{7,8},{8,7},{9,10},{10,9},{11,... | collective-permute-start | bytes 196616 | tf_op jit(solution)/shard_map/ppermute | solution.py:712
  73.6 4.2 %collective-permute-start.13 = (f32[16,8,128]{2,1,0:T(8,128)S(1)}, f32[16,8,128]{2,1,0:T(8,128)S(1)}, u32[]{:S(2)}, u32[]{:S(2)}) collective-permute-start(f32[16,8,128]{2,1,0:T(8,128)S(1)} %get-tuple-element.63), channel_id=1, source_target_pairs={{0,1},{1,0},{2,3},{3,2},{4,5},{5,4},{6,7},{7,6},{8,9},{9,8},{10,11... | collective-permute-start | bytes 196616 | tf_op jit(solution)/shard_map/ppermute | solution.py:712
  78.8 10.8 %collective-permute-start.14 = (f32[250,128]{1,0:T(8,128)S(1)}, f32[250,128]{1,0:T(8,128)S(1)}, u32[]{:S(2)}, u32[]{:S(2)}) collective-permute-start(f32[250,128]{1,0:T(8,128)S(1)} %get-tuple-element.66), channel_id=1, source_target_pairs={{0,64},{64,0},{128,192},{192,128},{1,65},{65,1},{129,193},{193,129... | collective-permute-start | bytes 384008 | tf_op jit(solution)/shard_map/ppermute | solution.py:825
  87.2 5.0 %collective-permute-start.15 = (f32[250,128]{1,0:T(8,128)S(1)}, f32[250,128]{1,0:T(8,128)S(1)}, u32[]{:S(2)}, u32[]{:S(2)}) collective-permute-start(f32[250,128]{1,0:T(8,128)S(1)} %get-tuple-element.67), channel_id=1, source_target_pairs={{0,128},{64,192},{128,0},{192,64},{1,129},{65,193},{129,1},{193,65... | collective-permute-start | bytes 384008 | tf_op jit(solution)/shard_map/ppermute | solution.py:825
  87.2 8.0 %collective-permute-start.16 = (f32[250,128]{1,0:T(8,128)S(1)}, f32[250,128]{1,0:T(8,128)S(1)}, u32[]{:S(2)}, u32[]{:S(2)}) collective-permute-start(f32[250,128]{1,0:T(8,128)S(1)} %get-tuple-element.68), channel_id=1, source_target_pairs={{0,192},{64,128},{128,64},{192,0},{1,193},{65,129},{129,65},{193,1... | collective-permute-start | bytes 384008 | tf_op jit(solution)/shard_map/ppermute | solution.py:825
where the time goes:
time: 121 us
  starting transfers between devices  52.2 us (43%)
  waiting for transfers between devices  27.3 us (23%)
  blocking collectives  24.8 us (20%)
  Pallas kernels  11.3 us (9%)
  local copies, waits for them, and re-layouts  4.63 us (4%)
    all_to_all x1, blocking collectives, shards(): lax.all_to_all(jnp.broadcast_to(message[None], (devices, 1, 128)), everyo...  24.8 us
    ppermute x6, starting transfers between devices, across(): lax.ppermute(array, 'space', [(i, i ^ stride) for i in range(devices)])  19.3 us
    ppermute x3, starting transfers between devices, exchange(): lax.ppermute(near, 'space', near_pairs)  18.1 us
    ppermute x6, waiting for transfers between devices, across(): lax.ppermute(array, 'space', [(i, i ^ stride) for i in range(devices)])  15.5 us
    pallas_call x11, Pallas kernels, call(): pl.pallas_call(kernel, out_shape=[jax.ShapeDtypeStruct(shape, F32) for sh...  11.3 us
    ppermute x3, starting transfers between devices, shards(): lax.ppermute(pieces[k], 'event', [(i, i ^ k) for i in range(events)])  10.2 us
    ppermute x3, waiting for transfers between devices, shards(): lax.ppermute(pieces[k], 'event', [(i, i ^ k) for i in range(events)])  5.66 us
    unnamed x16, local copies, waits for them, and re-layouts  4.56 us
  transfers between devices with their start and end apart: 17, of which 10 were waited for; matrix products, arithmetic and copies ran while one was open for 0% of the time, Pallas kernels for 5%

commit v1 on v0

--- a/solution.py
+++ b/solution.py
@@ -283,31 +283,30 @@
                 emit(p, q * 4 + r, rows[r, pl.ds(32 * p + q, 8, stride=4), :])
 
 
-def load(sources, buffers, semaphores):
-    copies = [
-        pltpu.make_async_copy(source, buffer, semaphores.at[k])
-        for k, (source, buffer) in enumerate(zip(sources, buffers))
-    ]
-    for copy in copies:
-        copy.start()
-    return copies
-
-
-def first_kernel(
-    now_hbm, adjoint_hbm, u_out, lam_out, message, rows, now_ref, adjoint_ref, semaphores
-):
-    copies = load((now_hbm, adjoint_hbm), (now_ref, adjoint_ref), semaphores)
+def facts_kernel(receivers_ref, observed_ref, out):
+    out[0:1, :] = receivers_ref[...].astype(F32)
+    energy = jnp.zeros((1, 128), F32)
+    for step in range(3):
+        values = observed_ref[step]
+        energy = energy + values * values
+        if step < 2:
+            out[step + 1 : step + 2, :] = values
+    out[3:4, :] = energy
+
+
+def first_kernel(states_ref, facts_ref, u_out, lam_out, message, rows):
     sh = Shifts()
     near, far = selection(False), selection(True)
-    for which, (source, target) in enumerate(((now_ref, u_out), (adjoint_ref, lam_out))):
+    for which, target in enumerate((u_out, lam_out)):
 
         def emit(p, qr, v, target=target):
             target[p * 16 + qr] = v
 
-        copies[which].wait()
-        to_local(source, near, far, rows, emit)
+        to_local(states_ref.at[which], near, far, rows, emit)
         for k, v in enumerate(pack_low(sh, [target[qr] for qr in range(16)])):
             message[8 * which + k] = v
+    message[16] = jnp.zeros((8, 128), F32)
+    message[16, 0:4, :] = facts_ref[...]
 
 
 def receiver_rows(receivers):
@@ -325,41 +324,16 @@
 
 
 def second_kernel(
-    slab_ref,
-    prev_hbm,
-    next_hbm,
-    density_hbm,
-    modulus_hbm,
-    receivers_ref,
-    observed_ref,
-    prev_out,
-    next_out,
-    scale_out,
-    stiff_out,
-    counts_out,
-    message,
-    rows,
-    prev_ref,
-    next_ref,
-    density_ref,
-    modulus_ref,
-    semaphores,
+    slab_ref, fields_ref, modulus_ref, prev_out, next_out, scale_out, stiff_out, message, rows
 ):
-    copies = load(
-        (prev_hbm, next_hbm, density_hbm, modulus_hbm),
-        (prev_ref, next_ref, density_ref, modulus_ref),
-        semaphores,
-    )
     sh = Shifts()
-    sub, lane = iotas()
     near, far = selection(False), selection(True)
-    for which, (source, target) in enumerate(((prev_ref, prev_out), (next_ref, next_out))):
+    for which, target in enumerate((prev_out, next_out)):
 
         def emit(p, qr, v, target=target):
             target[p * 16 + qr] = v
 
-        copies[which].wait()
-        to_local(source, near, far, rows, emit)
+        to_local(fields_ref.at[which], near, far, rows, emit)
     line = (0.2, 49.0 / 90.0, 32.0 / 45.0, 49.0 / 90.0)
     first_x = jnp.logical_and(sh.low, slab_ref[0] == 0)
 
@@ -370,9 +344,7 @@
         mass = mass * (jnp.where(sh.lane_first, 0.1, 0.2).astype(F32) if r == 0 else line[r])
         scale_out[p * 16 + qr] = (TIME_STEP * TIME_STEP) / mass
 
-    copies[2].wait()
-    to_local(density_ref, near, far, rows, emit_scale)
-    copies[3].wait()
+    to_local(fields_ref.at[2], near, far, rows, emit_scale)
     for p in range(5):
         for q in range(5):
             for r in range(5):
@@ -381,30 +353,39 @@
                     [modulus_ref[p, 0, q, r], modulus_ref[p, 1, q, r]], axis=0
                 )
                 stiff_out[p * 25 + q * 5 + r] = weight * block
-    row_hot, lane_hot = one_hots(receivers_ref[...])
-    row_hot = jnp.where(row_hot, 1.0, 0.0).astype(BF16)
-    ones = jnp.where(lane_hot, 1.0, 0.0)
+    for which, field in enumerate((prev_out, next_out, scale_out)):
+        for k, v in enumerate(pack_low(sh, [field[qr] for qr in range(16)])):
+            message[8 * which + k] = v
+
+
+def count_kernel(receivers_ref, observed_ref, message, counts_out, far_out):
     contract = (((1,), (1,)), ((), ()))
 
-    def put_counts(which, total):
+    def counted(receivers, observed, nodes):
+        row, lane = receiver_rows(receivers)
+        row_hot = lax.broadcasted_iota(jnp.int32, (nodes, 128), 0) == row
+        row_hot = jnp.where(row_hot, 1.0, 0.0).astype(BF16)
+        lane_hot = lax.broadcasted_iota(jnp.int32, (128, 128), 0) == lane
+        ones = jnp.where(lane_hot, 1.0, 0.0).astype(BF16)
+        totals = [lax.dot_general(row_hot, ones, contract, preferred_element_type=F32)]
+        for values in observed:
+            total = None
+            for part in split3(jnp.where(lane_hot, values, 0.0)):
+                t = lax.dot_general(row_hot, part, contract, preferred_element_type=F32)
+                total = t if total is None else total + t
+            totals.append(total)
+        return totals
+
+    own = counted(receivers_ref[...], [observed_ref[0], observed_ref[1]], 512)
+    for which, total in enumerate(own):
         for n in range(64):
             counts_out[which * 64 + n] = total[8 * n : 8 * n + 8]
-
-    put_counts(
-        0, lax.dot_general(row_hot, ones.astype(BF16), contract, preferred_element_type=F32)
-    )
-    for step in range(2):
-        spread = jnp.where(lane_hot, observed_ref[step], 0.0)
-        total = None
-        for part in split3(spread):
-            t = lax.dot_general(row_hot, part, contract, preferred_element_type=F32)
-            total = t if total is None else total + t
-        put_counts(1 + step, total)
-    sources = [(prev_out, 0), (next_out, 0), (scale_out, 0)]
-    sources += [(counts_out, 0), (counts_out, 64), (counts_out, 128)]
-    for which, (field, base) in enumerate(sources):
-        for k, v in enumerate(pack_low(sh, [field[base + qr] for qr in range(16)])):
-            message[8 * which + k] = v
+    theirs = counted(
+        message[16, 0:1, :].astype(jnp.int32), [message[16, 1:2, :], message[16, 2:3, :]], 128
+    )
+    for which, total in enumerate(theirs):
+        for n in range(16):
+            far_out[which * 16 + n] = half_turn(total[8 * n : 8 * n + 8])
 
 
 def without_far(sh, field):
@@ -476,6 +457,7 @@
     lam1_out,
     scale_out,
     u1_force,
+    lam1_force,
     far,
     near,
     blocks,
@@ -495,117 +477,154 @@
             scale_out[p * 16 + qr] = s
             u1_out[p * 16 + qr] = 2.0 * u0(p, qr) - before(p, qr) - s * u_total(p, qr)
             lam1_out[p * 16 + qr] = 2.0 * lam2(p, qr) - after(p, qr) - s * lam_total(p, qr)
-    expand(sh, stored(u1_out), blocks)
-    force(sh, blocks, stiff, scratch, u1_force)
-    put_messages(sh, odd, u1_force, far, near, 0)
+    for which, (field, out) in enumerate(((u1_out, u1_force), (lam1_out, lam1_force))):
+        expand(sh, stored(field), blocks)
+        force(sh, blocks, stiff, scratch, out)
+        put_messages(sh, odd, out, far, near, 8 * which)
 
 
 def mean_square(energy):
-    total = jnp.sum(energy, axis=1, keepdims=True)
+    total = jnp.sum(energy[3:4], axis=1, keepdims=True)
     return total / SAMPLES + EPSILON
 
 
 def step_two_kernel(
     slab_ref,
-    energy_ref,
     u_ref,
+    lam_ref,
     message0,
-    message1,
     u1_ref,
     lam1_ref,
     scale,
     counts,
+    far_counts,
     stiff,
     u1_force,
+    lam1_force,
     far_in,
     near_in,
     u2_out,
-    lam1_out,
+    driven1_out,
+    lam0_out,
     source_out,
-    u2_force,
-    lam1_force,
+    driven1_force,
     far,
     near,
     blocks,
     scratch,
 ):
+    u2_force = u2_out.at[pl.ds(80, 80)]
     sh = Shifts()
     odd = is_odd(slab_ref)
     incoming = Incoming(odd, far_in, near_in)
-    inverse = jnp.broadcast_to(1.0 / mean_square(energy_ref[...]), (8, 128))
-    u0 = extended(sh, u_ref, message0, 0)
-    count = extended(sh, counts.at[pl.ds(0, 64)], message1, 24)
-    seen = [extended(sh, counts.at[pl.ds(64 + 64 * n, 64)], message1, 32 + 8 * n) for n in range(2)]
-    total = assembled(sh, u1_force, incoming, 0)
+    u0, lam2 = extended(sh, u_ref, message0, 0), extended(sh, lam_ref, message0, 8)
+
+    def nodal(which):
+        def get(p, qr):
+            if p < 4:
+                return counts[64 * which + p * 16 + qr]
+            return jnp.where(
+                sh.low, half_turn(counts[64 * which + qr]), far_counts[16 * which + qr]
+            )
+
+        return get
+
+    count, seen = nodal(0), (nodal(1), nodal(2))
+    u_total = assembled(sh, u1_force, incoming, 0)
+    lam_total = assembled(sh, lam1_force, incoming, 8)
     for p in range(5):
         for qr in range(16):
             at = p * 16 + qr
             s, u1, c = scale[at], u1_ref[at], count(p, qr)
-            u2 = 2.0 * u1 - u0(p, qr) - s * total(p, qr)
+            u2 = 2.0 * u1 - u0(p, qr) - s * u_total(p, qr)
             u2_out[at] = u2
-            lam1_out[at] = lam1_ref[at] + s * ((c * u2 - seen[1](p, qr)) * inverse)
-            source_out[at] = s * ((c * u1 - seen[0](p, qr)) * inverse)
-    expand(sh, stored(lam1_out), blocks)
-    force(sh, blocks, stiff, scratch, lam1_force)
-    put_messages(sh, odd, lam1_force, far, near, 0)
-    expand(sh, stored(u2_out), blocks)
-    force(sh, blocks, stiff, scratch, u2_force)
-    put_messages(sh, odd, u2_force, far, near, 8)
-
-
-def middle_kernel(u1_ref, lam1_ref, u2_ref, lam_ref, message0, acc, first, second):
+            driven1_out[at] = s * (c * u2 - seen[1](p, qr))
+            source_out[at] = s * (c * u1 - seen[0](p, qr))
+            lam0_out[at] = 2.0 * lam1_ref[at] - lam2(p, qr) - s * lam_total(p, qr)
+    pairs = ((driven1_out, driven1_force), (u2_out, u2_force))
+    for which, (field, out) in enumerate(pairs):
+        expand(sh, stored(field), blocks)
+        force(sh, blocks, stiff, scratch, out)
+        put_messages(sh, odd, out, far, near, 8 * which)
+
+
+def middle_kernel(
+    u_ref,
+    lam_ref,
+    message0,
+    u1_ref,
+    lam1_ref,
+    u2_ref,
+    driven1_ref,
+    lam0_ref,
+    scale,
+    acc,
+    driven_acc,
+    u3_out,
+    first,
+    second,
+):
     sh = Shifts()
+    for at in range(64):
+        f = u2_ref[80 + at]
+        if at < 16:
+            f = f + jnp.where(sh.low, 0.0, half_turn(u2_ref[144 + at]))
+        u3_out[at] = 2.0 * u2_ref[at] - u1_ref[at] - scale[at] * f
     expand(sh, stored(u1_ref), first)
+    expand(sh, stored(driven1_ref), second)
+    products(first, second, driven_acc, True)
     expand(sh, stored(lam1_ref), second)
     products(first, second, acc, True)
     expand(sh, stored(u2_ref), first)
     expand(sh, extended(sh, lam_ref, message0, 8), second)
     products(first, second, acc, False)
+    expand(sh, extended(sh, u_ref, message0, 0), first)
+    expand(sh, stored(lam0_ref), second)
+    products(first, second, acc, False)
 
 
 def last_kernel(
     slab_ref,
     event_ref,
+    energy_ref,
     u_ref,
-    lam_ref,
     message0,
-    lam1_ref,
+    driven1_ref,
     scale,
     source,
-    lam1_force,
+    driven1_force,
     far_in,
     near_in,
     acc_ref,
+    driven_acc_ref,
     out0,
     out1,
     out2,
     out3,
-    lam0,
+    driven0,
     first,
     second,
     acc,
     flat,
 ):
     sh = Shifts()
-    lam2 = extended(sh, lam_ref, message0, 8)
-    total = assembled(sh, lam1_force, Incoming(is_odd(slab_ref), far_in, near_in), 0)
+    total = assembled(sh, driven1_force, Incoming(is_odd(slab_ref), far_in, near_in), 0)
     for p in range(5):
         for qr in range(16):
             at = p * 16 + qr
-            lam0[at] = (
-                2.0 * lam1_ref[at] - lam2(p, qr) - scale[at] * total(p, qr) + source[at]
-            )
+            driven0[at] = 2.0 * driven1_ref[at] - scale[at] * total(p, qr) + source[at]
     expand(sh, extended(sh, u_ref, message0, 0), first)
-    expand(sh, stored(lam0), second)
+    expand(sh, stored(driven0), second)
     for i in range(125):
-        acc[i] = acc_ref[i]
+        acc[i] = driven_acc_ref[i]
     products(first, second, acc, False)
+    inverse = jnp.broadcast_to(1.0 / mean_square(energy_ref[...]), (8, 128))
     for p in range(5):
         for q in range(5):
             for r in range(5):
                 at = p * 25 + q * 5 + r
                 weight = float(-WEIGHTS[p] * WEIGHTS[q] * WEIGHTS[r])
-                v = weight * acc[at]
+                v = weight * (acc_ref[at] + inverse * acc[at])
                 for i in range(2):
                     row = 4 * ((2 * p + i) * 25 + q * 5 + r)
                     flat[row : row + 4, :] = v[4 * i : 4 * i + 4]
@@ -620,19 +639,20 @@
     observed_ref,
     u1_ref,
     u2_ref,
+    u3_ref,
     scale,
-    u2_force,
     far_in,
     near_in,
     out,
     u3,
 ):
     sh = Shifts()
-    total = assembled(sh, u2_force, Incoming(is_odd(slab_ref), far_in, near_in), 8)
-    for p in range(4):
-        for qr in range(16):
-            at = p * 16 + qr
-            u3[at] = 2.0 * u2_ref[at] - u1_ref[at] - scale[at] * total(p, qr)
+    incoming = Incoming(is_odd(slab_ref), far_in, near_in)
+    for at in range(64):
+        v = u3_ref[at]
+        if at < 16:
+            v = v - scale[at] * jnp.where(sh.low, incoming.from_left(8, at), 0.0)
+        u3[at] = v
     row_hot, lane_hot = one_hots(receivers_ref[...])
     row_hot = jnp.where(row_hot, 1.0, 0.0).astype(BF16)
     squares = jnp.zeros((1, 128), F32)
@@ -674,23 +694,18 @@
 
 
 COST = 16 << 20
-VMEM_GRANT = 16 << 20
+VMEM_GRANT = 8 << 20
 VMEM_SPEC = pl.BlockSpec(memory_space=pltpu.VMEM)
-HBM_SPEC = pl.BlockSpec(memory_space=pltpu.MemorySpace.HBM)
 SMEM_SPEC = pl.BlockSpec(memory_space=pltpu.SMEM)
 
 
-def call(kernel, args, outs, scratch=(), scalars=0, loads=0):
-    buffers = [pltpu.VMEM(arg.shape, F32) for arg in args[scalars : scalars + loads]]
-    semaphores = [pltpu.SemaphoreType.DMA((loads,))] if loads else []
+def call(kernel, args, outs, scratch=(), scalars=0):
     return pl.pallas_call(
         kernel,
         out_shape=[jax.ShapeDtypeStruct(shape, F32) for shape in outs],
-        in_specs=[SMEM_SPEC] * scalars
-        + [HBM_SPEC] * loads
-        + [VMEM_SPEC] * (len(args) - scalars - loads),
+        in_specs=[SMEM_SPEC] * scalars + [VMEM_SPEC] * (len(args) - scalars),
         out_specs=[VMEM_SPEC] * len(outs),
-        scratch_shapes=[pltpu.VMEM(shape, F32) for shape in scratch] + buffers + semaphores,
+        scratch_shapes=[pltpu.VMEM(shape, F32) for shape in scratch],
         cost_estimate=pl.CostEstimate(flops=0, bytes_accessed=COST, transcendentals=0),
         compiler_params=pltpu.CompilerParams(vmem_limit_bytes=VMEM_GRANT),
     )(*args)
@@ -700,21 +715,25 @@
     return (count, 8, 128)
 
 
+def send(array, axis, pairs):
+    return lax.ppermute(array, axis, pairs)
+
+
 def to_left(array):
     devices = lax.axis_size("space")
-    return lax.ppermute(array, "space", [(i, i - 1) for i in range(1, devices)])
+    return send(array, "space", [(i, i - 1) for i in range(1, devices)])
 
 
 def exchange(far, near):
     devices = lax.axis_size("space")
     far_pairs = [(i, i + 1 if i % 2 else i - 1) for i in range(1, devices - 1)]
     near_pairs = [(i, i - 1 if i % 2 else i + 1) for i in range(devices)]
-    return (lax.ppermute(far, "space", far_pairs), lax.ppermute(near, "space", near_pairs))
+    return (send(far, "space", far_pairs), send(near, "space", near_pairs))
 
 
 def across(array, stride):
     devices = lax.axis_size("space")
-    return array + lax.ppermute(array, "space", [(i, i ^ stride) for i in range(devices)])
+    return array + send(array, "space", [(i, i ^ stride) for i in range(devices)])
 
 
 def shards(state_now, state_prev, adjoint_now, adjoint_next, modulus, density, receivers, observed):
@@ -724,35 +743,35 @@
     observed = jnp.transpose(observed, (1, 0, 2))
     modulus = jnp.transpose(modulus, (0, 1, 2, 4, 3, 5))
 
-    energy = jnp.sum(observed * observed, axis=0)
-    energy = across(energy, 1)
+    (facts,) = call(facts_kernel, (receivers, observed), [(4, 128)])
+    energy = across(facts, 1)
 
     u0, lam2, planes = call(
         first_kernel,
-        (state_now[0], adjoint_now[0]),
-        [vectors(64), vectors(64), vectors(16)],
+        (jnp.stack([state_now[0], adjoint_now[0]]), facts),
+        [vectors(64), vectors(64), vectors(17)],
         [(4, 128, 128)],
-        loads=2,
-    )
+    )
+    message0 = to_left(planes)
     energy = across(energy, 16)
-    message0 = to_left(planes)
-    before, after, scale, stiff, counts, planes = call(
+    before, after, scale, stiff, planes = call(
         second_kernel,
-        (slab, state_prev[0], adjoint_next[0], density, modulus, receivers, observed),
-        [vectors(64), vectors(64), vectors(64), vectors(125), vectors(192), vectors(48)],
+        (slab, jnp.stack([state_prev[0], adjoint_next[0], density]), modulus),
+        [vectors(64), vectors(64), vectors(64), vectors(125), vectors(24)],
         [(4, 128, 128)],
         scalars=1,
-        loads=4,
-    )
-    energy = across(energy, 2)
-    message1 = to_left(planes)
+    )
     u_force, lam_force = call(
         force_kernel,
         (u0, lam2, stiff),
         [vectors(80), vectors(80)],
         [vectors(125), vectors(125)],
     )
-    energy = across(energy, 32)
+    message1 = to_left(planes)
+    energy = across(energy, 2)
+    counts, far_counts = call(
+        count_kernel, (receivers, observed, message0), [vectors(192), vectors(48)]
+    )
     u_force, lam_force, far, near = call(
         far_plane_kernel,
         (slab, message0, stiff, u_force, lam_force),
@@ -760,9 +779,9 @@
         [vectors(125)],
         scalars=1,
     )
-    energy = across(energy, 4)
+    energy = across(energy, 32)
     far, near = exchange(far, near)
-    u1, lam1, scale, u1_force, far, near = call(
+    u1, lam1, scale, u1_force, lam1_force, far, near = call(
         step_one_kernel,
         (
             slab,
@@ -779,55 +798,68 @@
             far,
             near,
         ),
-        [vectors(80)] * 4 + [vectors(8)] * 2,
+        [vectors(80)] * 5 + [vectors(16)] * 2,
         [vectors(125), vectors(125)],
         scalars=1,
     )
+    energy = across(energy, 4)
     energy = across(energy, 8)
     far, near = exchange(far, near)
-    u2, lam1, source, u2_force, lam1_force, far, near = call(
+    u2, driven1, lam0, source, driven1_force, far, near = call(
         step_two_kernel,
         (
             slab,
-            energy,
             u0,
+            lam2,
             message0,
-            message1,
             u1,
             lam1,
             scale,
             counts,
+            far_counts,
             stiff,
             u1_force,
+            lam1_force,
             far,
             near,
         ),
-        [vectors(80)] * 5 + [vectors(16)] * 2,
+        [vectors(160)] + [vectors(80)] * 4 + [vectors(16)] * 2,
         [vectors(125), vectors(125)],
         scalars=1,
     )
     far, near = exchange(far, near)
-    (acc,) = call(
+    acc, driven_acc, u3 = call(
         middle_kernel,
-        (u1, lam1, u2, lam2, message0),
-        [vectors(125)],
+        (u0, lam2, message0, u1, lam1, u2, driven1, lam0, scale),
+        [vectors(125), vectors(125), vectors(64)],
         [vectors(125), vectors(125)],
     )
     pieces = call(
         last_kernel,
-        (slab, event, u0, lam2, message0, lam1, scale, source, lam1_force, far, near, acc),
+        (
+            slab,
+            event,
+            energy,
+            u0,
+            message0,
+            driven1,
+            scale,
+            source,
+            driven1_force,
+            far,
+            near,
+            acc,
+            driven_acc,
+        ),
         [(250, 128)] * 4,
         [vectors(80), vectors(125), vectors(125), vectors(125), (1000, 128)],
         scalars=2,
     )
     events = lax.axis_size("event")
-    others = [
-        lax.ppermute(pieces[k], "event", [(i, i ^ k) for i in range(events)])
-        for k in (1, 2, 3)
-    ]
+    others = [send(pieces[k], "event", [(i, i ^ k) for i in range(events)]) for k in (1, 2, 3)]
     (squares,) = call(
         misfit_kernel,
-        (slab, receivers, observed, u1, u2, scale, u2_force, far, near),
+        (slab, receivers, observed, u1, u2, u3, scale, far, near),
         [(1, 128)],
         [vectors(64)],
         scalars=1,

time: 121 us -> 120 us (level)
  starting transfers between devices: 52.2 us -> 57.7 us
  blocking collectives: 24.8 us -> 20.2 us
  waiting for transfers between devices: 27.3 us -> 23.2 us
  Pallas kernels: 11.3 us -> 14.4 us
  local copies, waits for them, and re-layouts: 4.63 us -> 1.72 us
  other arithmetic: 0.04 us -> 1.84 us
    ppermute x17, starting transfers between devices: 52.2 us -> 57.7 us  [send(): return lax.ppermute(array, axis, pairs)]
    all_to_all x1, blocking collectives: 24.8 us -> 20.2 us  [shards(): lax.all_to_all(jnp.broadcast_to(message[None], (devices, 1, 128)), everyo...]
    ppermute x17, waiting for transfers between devices: 27.3 us -> 23.2 us  [send(): return lax.ppermute(array, axis, pairs)]
    pallas_call x11 -> x13, Pallas kernels: 11.3 us -> 14.4 us  [call(): pl.pallas_call(kernel, out_shape=[jax.ShapeDtypeStruct(shape, F32) for sh...]
    unnamed x16 -> x12, local copies, waits for them, and re-layouts: 4.56 us -> 1.65 us
  transfers between devices with their start and end apart: 17 -> 17, of which waited for: 10 -> 10; matrix products, arithmetic and copies ran while one was open for 0% -> 1% of each run, Pallas kernels for 5% -> 6%
where the time goes in v1:
time: 120 us
  starting transfers between devices  57.7 us (48%)
  waiting for transfers between devices  23.2 us (19%)
  blocking collectives  20.2 us (17%)
  Pallas kernels  14.4 us (12%)
  other arithmetic  1.84 us (2%)
  local copies, waits for them, and re-layouts  1.72 us (1%)
    ppermute x17, starting transfers between devices, send(): return lax.ppermute(array, axis, pairs)  57.7 us
    ppermute x17, waiting for transfers between devices, send(): return lax.ppermute(array, axis, pairs)  23.2 us
    all_to_all x1, blocking collectives, shards(): lax.all_to_all(jnp.broadcast_to(message[None], (devices, 1, 128)), everyo...  20.2 us
    pallas_call x13, Pallas kernels, call(): pl.pallas_call(kernel, out_shape=[jax.ShapeDtypeStruct(shape, F32) for sh...  14.4 us
  transfers between devices with their start and end apart: 17, of which 10 were waited for; matrix products, arithmetic and copies ran while one was open for 1% of the time, Pallas kernels for 6%

profile of v1, /device:TPU:1, one launch (start us, length us, event | category | flops | bytes accessed | tf_op | source)
XLA Modules:
  0.0 120.0 jit_solution(2521297190049422713)
XLA Ops:
  0.6 0.0 copy-start.1
  0.6 0.0 copy-start.2
  0.6 0.7 copy-done.1
  1.3 0.0 copy-done.2
  1.3 0.0 copy-start.5
  1.3 1.1 pad_maximum_fusion.1.states_ref
  2.4 0.0 copy-start.3
  2.5 0.0 copy-start.4
  2.5 0.5 shard_map.96
  3.0 1.3 %collective-permute-start.6 = (f32[17,8,128]{2,1,0:T(8,128)S(1)}, f32[17,8,128]{2,1,0:T(8,128)S(1)}, u32[]{:S(2)}, u32[]{:S(2)}) collective-permute-start(f32[17,8,128]{2,1,0:T(8,128)S(1)} %get-tuple-element.44), channel_id=1, source_target_pairs={{1,0},{2,1},{3,2},{4,3},{5,4},{6,5},{7,6},{8,7},{9,8},{10,9},{11,1... | collective-permute-start | bytes 208904 | tf_op jit(solution)/shard_map/ppermute | solution.py:719
  4.3 0.0 copy-done.5
  4.3 0.0 copy-done.3
  4.3 0.0 copy-done.4
  4.3 0.0 copy-start
  4.3 0.1 pad_maximum_fusion.fields_ref
  4.4 1.0 copy-done
  5.3 0.7 shard_map.97
  6.1 1.3 %collective-permute-start.7 = (f32[24,8,128]{2,1,0:T(8,128)S(1)}, f32[24,8,128]{2,1,0:T(8,128)S(1)}, u32[]{:S(2)}, u32[]{:S(2)}) collective-permute-start(f32[24,8,128]{2,1,0:T(8,128)S(1)} %get-tuple-element.50), channel_id=1, source_target_pairs={{1,0},{2,1},{3,2},{4,3},{5,4},{6,5},{7,6},{8,7},{9,8},{10,9},{11,1... | collective-permute-start | bytes 294920 | tf_op jit(solution)/shard_map/ppermute | solution.py:719
  7.4 1.4 %shard_map.98 = (f32[80,8,128]{2,1,0:T(8,128)S(1)}, f32[80,8,128]{2,1,0:T(8,128)S(1)}) custom-call(f32[64,8,128]{2,1,0:T(8,128)S(1)} %get-tuple-element.43.u_ref, f32[64,8,128]{2,1,0:T(8,128)S(1)} %get-tuple-element.45.lam_ref, f32[125,8,128]{2,1,0:T(8,128)S(1)} %get-tuple-element.49.stiff), custom_call_target="tpu_custom_call" | custom-call | bytes 16777216 | tf_op jit(solution)/shard_map/pallas_call | solution.py:703
  8.8 0.0 collective-permute-done.6.message.message0
  8.8 0.4 shard_map.99
  9.2 0.7 collective-permute-start.8
  9.9 6.2 %collective-permute-start.9 = (f32[16,8,128]{2,1,0:T(8,128)S(1)}, f32[16,8,128]{2,1,0:T(8,128)S(1)}, u32[]{:S(2)}, u32[]{:S(2)}) collective-permute-start(f32[16,8,128]{2,1,0:T(8,128)S(1)} %get-tuple-element.56), channel_id=1, source_target_pairs={{0,1},{1,0},{2,3},{3,2},{4,5},{5,4},{6,7},{7,6},{8,9},{9,8},{10,11... | collective-permute-start | bytes 196616 | tf_op jit(solution)/shard_map/ppermute | solution.py:719
  16.1 0.0 collective-permute-done.7.message1
  16.1 0.0 collective-permute-done.8.far_in
  16.1 1.6 %collective-permute-done.9.near_in = f32[16,8,128]{2,1,0:T(8,128)S(1)} collective-permute-done((f32[16,8,128]{2,1,0:T(8,128)S(1)}, f32[16,8,128]{2,1,0:T(8,128)S(1)}, u32[]{:S(2)}, u32[]{:S(2)}) %collective-permute-start.9) | collective-permute-done | bytes 65568 | tf_op jit(solution)/shard_map/ppermute | solution.py:719
  17.7 1.6 %shard_map.100 = (f32[80,8,128]{2,1,0:T(8,128)S(1)}, f32[80,8,128]{2,1,0:T(8,128)S(1)}, f32[80,8,128]{2,1,0:T(8,128)S(1)}, f32[80,8,128]{2,1,0:T(8,128)S(1)}, f3...) custom-call(s32[1]{0:T(128)} %bitcast.1.slab_ref, ...), custom_call_target="tpu_custom_call" | custom-call | bytes 16777216 | tf_op jit(solution)/shard_map/pallas_call | solution.py:703
  19.3 0.7 collective-permute-start.10
  20.0 7.1 %collective-permute-start.11 = (f32[16,8,128]{2,1,0:T(8,128)S(1)}, f32[16,8,128]{2,1,0:T(8,128)S(1)}, u32[]{:S(2)}, u32[]{:S(2)}) collective-permute-start(f32[16,8,128]{2,1,0:T(8,128)S(1)} %get-tuple-element.65), channel_id=1, source_target_pairs={{0,1},{1,0},{2,3},{3,2},{4,5},{5,4},{6,7},{7,6},{8,9},{9,8},{10,11... | collective-permute-start | bytes 196616 | tf_op jit(solution)/shard_map/ppermute | solution.py:719
  27.1 0.6 shard_map.101
  27.6 0.0 collective-permute-done.10.far_in
  27.6 1.1 collective-permute-done.11.near_in
  28.7 2.4 %shard_map.102 = (f32[160,8,128]{2,1,0:T(8,128)S(1)}, f32[80,8,128]{2,1,0:T(8,128)S(1)}, f32[80,8,128]{2,1,0:T(8,128)S(1)}, f32[80,8,128]{2,1,0:T(8,128)S(1)}, f...) custom-call(s32[1]{0:T(128)} %bitcast.1.slab_ref, ...), custom_call_target="tpu_custom_call" | custom-call | bytes 16777216 | tf_op jit(solution)/shard_map/pallas_call | solution.py:703
  31.1 1.3 %collective-permute-start.12 = (f32[16,8,128]{2,1,0:T(8,128)}, f32[16,8,128]{2,1,0:T(8,128)}, u32[]{:S(2)}, u32[]{:S(2)}) collective-permute-start(f32[16,8,128]{2,1,0:T(8,128)} %get-tuple-element.69), channel_id=1, source_target_pairs={{1,2},{2,1},{3,4},{4,3},{5,6},{6,5},{7,8},{8,7},{9,10},{10,9},{11,... | collective-permute-start | bytes 196616 | tf_op jit(solution)/shard_map/ppermute | solution.py:719
  32.4 5.2 %collective-permute-start.13 = (f32[16,8,128]{2,1,0:T(8,128)}, f32[16,8,128]{2,1,0:T(8,128)}, u32[]{:S(2)}, u32[]{:S(2)}) collective-permute-start(f32[16,8,128]{2,1,0:T(8,128)} %get-tuple-element.70), channel_id=1, source_target_pairs={{0,1},{1,0},{2,3},{3,2},{4,5},{5,4},{6,7},{7,6},{8,9},{9,8},{10,11... | collective-permute-start | bytes 196616 | tf_op jit(solution)/shard_map/ppermute | solution.py:719
  37.6 0.1 collective-permute-start
  37.7 2.3 %collective-permute-done = f32[4,128]{1,0:T(4,128)S(1)} collective-permute-done((f32[4,128]{1,0:T(4,128)S(1)}, f32[4,128]{1,0:T(4,128)S(1)}, u32[]{:S(2)}, u32[]{:S(2)}) %collective-permute-start) | collective-permute-done | bytes 2080 | tf_op jit(solution)/shard_map/ppermute | solution.py:719
  40.0 13.8 %collective-permute-start.1 = (f32[4,128]{1,0:T(4,128)S(1)}, f32[4,128]{1,0:T(4,128)S(1)}, u32[]{:S(2)}, u32[]{:S(2)}) collective-permute-start(f32[4,128]{1,0:T(4,128)S(1)} %add.18), channel_id=1, source_target_pairs={{0,16},{1,17},{2,18},{3,19},{4,20},{5,21},{6,22},{7,23},{8,24},{9,... | collective-permute-start | bytes 6152 | tf_op jit(solution)/shard_map/ppermute | solution.py:719
  53.8 1.0 collective-permute-done.1
  54.8 0.0 collective-permute-start.2
  54.8 3.9 %collective-permute-done.2 = f32[4,128]{1,0:T(4,128)S(1)} collective-permute-done((f32[4,128]{1,0:T(4,128)S(1)}, f32[4,128]{1,0:T(4,128)S(1)}, u32[]{:S(2)}, u32[]{:S(2)}) %collective-permute-start.2) | collective-permute-done | bytes 2080 | tf_op jit(solution)/shard_map/ppermute | solution.py:719
  58.7 3.4 %collective-permute-start.3 = (f32[4,128]{1,0:T(4,128)S(1)}, f32[4,128]{1,0:T(4,128)S(1)}, u32[]{:S(2)}, u32[]{:S(2)}) collective-permute-start(f32[4,128]{1,0:T(4,128)S(1)} %add.20), channel_id=1, source_target_pairs={{0,32},{1,33},{2,34},{3,35},{4,36},{5,37},{6,38},{7,39},{8,40},{9,... | collective-permute-start | bytes 6152 | tf_op jit(solution)/shard_map/ppermute | solution.py:719
  62.1 1.0 collective-permute-done.3
  63.1 0.0 collective-permute-start.4
  63.1 3.3 %collective-permute-done.4 = f32[4,128]{1,0:T(4,128)S(1)} collective-permute-done((f32[4,128]{1,0:T(4,128)S(1)}, f32[4,128]{1,0:T(4,128)S(1)}, u32[]{:S(2)}, u32[]{:S(2)}) %collective-permute-start.4) | collective-permute-done | bytes 2080 | tf_op jit(solution)/shard_map/ppermute | solution.py:719
  66.5 2.3 %collective-permute-start.5 = (f32[4,128]{1,0:T(4,128)S(1)}, f32[4,128]{1,0:T(4,128)}, u32[]{:S(2)}, u32[]{:S(2)}) collective-permute-start(f32[4,128]{1,0:T(4,128)S(1)} %add.22), channel_id=1, source_target_pairs={{0,8},{1,9},{2,10},{3,11},{4,12},{5,13},{6,14},{7,15},{8,0},{9,1},... | collective-permute-start | bytes 6152 | tf_op jit(solution)/shard_map/ppermute | solution.py:719
  68.8 4.1 %collective-permute-done.5 = f32[4,128]{1,0:T(4,128)} collective-permute-done((f32[4,128]{1,0:T(4,128)S(1)}, f32[4,128]{1,0:T(4,128)}, u32[]{:S(2)}, u32[]{:S(2)}) %collective-permute-start.5) | collective-permute-done | bytes 2080 | tf_op jit(solution)/shard_map/ppermute | solution.py:719
  72.9 0.7 add.23.energy_ref
  73.6 2.6 %shard_map.103 = (f32[125,8,128]{2,1,0:T(8,128)S(1)}, f32[125,8,128]{2,1,0:T(8,128)S(1)}, f32[64,8,128]{2,1,0:T(8,128)S(1)}) custom-call(f32[64,8,128]{2,1,0:T(8,128)S(1)} %get-tuple-element.43.u_ref, f32[64,8,128]{2,1,0:T(8,128)S(1)} %get-tuple-element.45.lam_ref, f32[17,8,128]{2,1,0:T(8,128)S(1)} %collective-permute-done.6.message.message0, ...), custom_call_target="tpu_custom_call" | custom-call | bytes 16777216 | tf_op jit(solution)/shard_map/pallas_call | solution.py:703
  76.1 0.0 collective-permute-done.12.far_in
  76.1 0.0 collective-permute-done.13.near_in
  76.2 1.8 %shard_map.104 = (f32[250,128]{1,0:T(8,128)S(1)}, f32[250,128]{1,0:T(8,128)S(1)}, f32[250,128]{1,0:T(8,128)S(1)}, f32[250,128]{1,0:T(8,128)S(1)}) custom-call(s32[1]{0:T(128)} %bitcast.1.slab_ref, s32[1]{0:T(128)} %bitcast.event_ref, f32[4,128]{1,0:T(4,128)S(1)} %add.23.energy_ref, f32[64,8,128]{2,1,0:T(8,128)S(1)} %get-tuple-element.43.u_ref, ...), custom_call_target="tpu_custom_call" | custom-call | bytes 16777216 | tf_op jit(solution)/shard_map/pallas_call | solution.py:703
  78.0 12.7 %collective-permute-start.14 = (f32[250,128]{1,0:T(8,128)S(1)}, f32[250,128]{1,0:T(8,128)S(1)}, u32[]{:S(2)}, u32[]{:S(2)}) collective-permute-start(f32[250,128]{1,0:T(8,128)S(1)} %get-tuple-element.76), channel_id=1, source_target_pairs={{0,64},{64,0},{128,192},{192,128},{1,65},{65,1},{129,193},{193,129... | collective-permute-start | bytes 384008 | tf_op jit(solution)/shard_map/ppermute | solution.py:719
  90.7 0.0 collective-permute-start.15
  90.7 1.7 %collective-permute-start.16 = (f32[250,128]{1,0:T(8,128)S(1)}, f32[250,128]{1,0:T(8,128)S(1)}, u32[]{:S(2)}, u32[]{:S(2)}) collective-permute-start(f32[250,128]{1,0:T(8,128)S(1)} %get-tuple-element.78), channel_id=1, source_target_pairs={{0,192},{64,128},{128,64},{192,0},{1,193},{65,129},{129,65},{193,1... | collective-permute-start | bytes 384008 | tf_op jit(solution)/shard_map/ppermute | solution.py:719
  92.4 1.5 %shard_map.105.misfit = f32[1,128]{1,0:T(1,128)S(1)} custom-call(s32[1]{0:T(128)} %bitcast.1.slab_ref, s32[1,128]{1,0:T(1,128)S(1)} %bitcast.18, f32[3,1,128]{2,1,0:T(1,128)S(1)} %bitcast.15, f32[80,8,128]{2,1,0:T(8,128)S(1)} %get-tuple-element.57.u1_ref, f32[160,8,128]{2,1,0:T(8,128)S(1)} %get-tuple-element.71.u2_ref, ...), custom_call_target="tpu_custom_call" | custom-call | bytes 16777216 | tf_op jit(solution)/shard_map/pallas_call | solution.py:703
  93.9 0.0 collective-permute-done.14.b
  93.9 1.7 %collective-permute-done.15.c = f32[250,128]{1,0:T(8,128)S(1)} collective-permute-done((f32[250,128]{1,0:T(8,128)S(1)}, f32[250,128]{1,0:T(8,128)S(1)}, u32[]{:S(2)}, u32[]{:S(2)}) %collective-permute-start.15) | collective-permute-done | bytes 128032 | tf_op jit(solution)/shard_map/ppermute | solution.py:719
  95.7 3.1 %collective-permute-done.16.d = f32[250,128]{1,0:T(8,128)S(1)} collective-permute-done((f32[250,128]{1,0:T(8,128)S(1)}, f32[250,128]{1,0:T(8,128)S(1)}, u32[]{:S(2)}, u32[]{:S(2)}) %collective-permute-start.16) | collective-permute-done | bytes 128032 | tf_op jit(solution)/shard_map/ppermute | solution.py:719
  98.7 0.1 shard_map.106
  98.9 0.1 broadcast_in_dim.9
  98.9 20.2 %all_to_all.5 = f32[256,1,128]{2,1,0:T(1,128)S(1)} all-to-all(f32[256,1,128]{2,1,0:T(1,128)S(1)} %broadcast_in_dim.9), channel_id=1, replica_groups=mesh['event'=4,'space'=64] {'event','space'}, dimensions={0} | all-to-all | bytes 262144 | tf_op jit(solution)/shard_map/all_to_all | solution.py:872
  119.1 0.8 shard_map.107
  (6 shorter events, 0.0 us)
Async XLA Ops:
  0.6 0.7 copy-start.1
  0.6 0.7 copy-start.2
  1.3 3.0 %copy-start.5 = (f32[1,8,16,512]{3,2,1,0:T(8,128)S(1)}, f32[1,8,16,512]{3,2,1,0:T(8,128)}, u32[]{:S(2)}) copy-start(f32[1,8,16,512]{3,2,1,0:T(8,128)} %param.9) | copy-start | bytes 786436
  2.4 1.8 %copy-start.3 = (f32[8,16,512]{2,1,0:T(8,128)S(1)}, f32[8,16,512]{2,1,0:T(8,128)}, u32[]{:S(2)}) copy-start(f32[8,16,512]{2,1,0:T(8,128)} %param.13) | copy-start | bytes 786436
  2.5 1.8 %copy-start.4 = (f32[1,8,16,512]{3,2,1,0:T(8,128)S(1)}, f32[1,8,16,512]{3,2,1,0:T(8,128)}, u32[]{:S(2)}) copy-start(f32[1,8,16,512]{3,2,1,0:T(8,128)} %param.11) | copy-start | bytes 786436
  3.0 5.8 %collective-permute-start.6 = (f32[17,8,128]{2,1,0:T(8,128)S(1)}, f32[17,8,128]{2,1,0:T(8,128)S(1)}, u32[]{:S(2)}, u32[]{:S(2)}) collective-permute-start(f32[17,8,128]{2,1,0:T(8,128)S(1)} %get-tuple-element.44), channel_id=1, source_target_pairs={{1,0},{2,1},{3,2},{4,3},{5,4},{6,5},{7,6},{8,7},{9,8},{10,9},{11,1... | collective-permute-start | bytes 208904 | tf_op jit(solution)/shard_map/ppermute | solution.py:719
  4.3 1.0 copy-start
  6.1 10.0 %collective-permute-start.7 = (f32[24,8,128]{2,1,0:T(8,128)S(1)}, f32[24,8,128]{2,1,0:T(8,128)S(1)}, u32[]{:S(2)}, u32[]{:S(2)}) collective-permute-start(f32[24,8,128]{2,1,0:T(8,128)S(1)} %get-tuple-element.50), channel_id=1, source_target_pairs={{1,0},{2,1},{3,2},{4,3},{5,4},{6,5},{7,6},{8,7},{9,8},{10,9},{11,1... | collective-permute-start | bytes 294920 | tf_op jit(solution)/shard_map/ppermute | solution.py:719
  9.2 6.8 %collective-permute-start.8 = (f32[16,8,128]{2,1,0:T(8,128)S(1)}, f32[16,8,128]{2,1,0:T(8,128)S(1)}, u32[]{:S(2)}, u32[]{:S(2)}) collective-permute-start(f32[16,8,128]{2,1,0:T(8,128)S(1)} %get-tuple-element.55), channel_id=1, source_target_pairs={{1,2},{2,1},{3,4},{4,3},{5,6},{6,5},{7,8},{8,7},{9,10},{10,9},{11,... | collective-permute-start | bytes 196616 | tf_op jit(solution)/shard_map/ppermute | solution.py:719
  9.9 7.8 %collective-permute-start.9 = (f32[16,8,128]{2,1,0:T(8,128)S(1)}, f32[16,8,128]{2,1,0:T(8,128)S(1)}, u32[]{:S(2)}, u32[]{:S(2)}) collective-permute-start(f32[16,8,128]{2,1,0:T(8,128)S(1)} %get-tuple-element.56), channel_id=1, source_target_pairs={{0,1},{1,0},{2,3},{3,2},{4,5},{5,4},{6,7},{7,6},{8,9},{9,8},{10,11... | collective-permute-start | bytes 196616 | tf_op jit(solution)/shard_map/ppermute | solution.py:719
  19.3 8.3 %collective-permute-start.10 = (f32[16,8,128]{2,1,0:T(8,128)S(1)}, f32[16,8,128]{2,1,0:T(8,128)S(1)}, u32[]{:S(2)}, u32[]{:S(2)}) collective-permute-start(f32[16,8,128]{2,1,0:T(8,128)S(1)} %get-tuple-element.64), channel_id=1, source_target_pairs={{1,2},{2,1},{3,4},{4,3},{5,6},{6,5},{7,8},{8,7},{9,10},{10,9},{11,... | collective-permute-start | bytes 196616 | tf_op jit(solution)/shard_map/ppermute | solution.py:719
  20.0 8.7 %collective-permute-start.11 = (f32[16,8,128]{2,1,0:T(8,128)S(1)}, f32[16,8,128]{2,1,0:T(8,128)S(1)}, u32[]{:S(2)}, u32[]{:S(2)}) collective-permute-start(f32[16,8,128]{2,1,0:T(8,128)S(1)} %get-tuple-element.65), channel_id=1, source_target_pairs={{0,1},{1,0},{2,3},{3,2},{4,5},{5,4},{6,7},{7,6},{8,9},{9,8},{10,11... | collective-permute-start | bytes 196616 | tf_op jit(solution)/shard_map/ppermute | solution.py:719
  31.1 45.0 %collective-permute-start.12 = (f32[16,8,128]{2,1,0:T(8,128)}, f32[16,8,128]{2,1,0:T(8,128)}, u32[]{:S(2)}, u32[]{:S(2)}) collective-permute-start(f32[16,8,128]{2,1,0:T(8,128)} %get-tuple-element.69), channel_id=1, source_target_pairs={{1,2},{2,1},{3,4},{4,3},{5,6},{6,5},{7,8},{8,7},{9,10},{10,9},{11,... | collective-permute-start | bytes 196616 | tf_op jit(solution)/shard_map/ppermute | solution.py:719
  32.4 43.8 %collective-permute-start.13 = (f32[16,8,128]{2,1,0:T(8,128)}, f32[16,8,128]{2,1,0:T(8,128)}, u32[]{:S(2)}, u32[]{:S(2)}) collective-permute-start(f32[16,8,128]{2,1,0:T(8,128)} %get-tuple-element.70), channel_id=1, source_target_pairs={{0,1},{1,0},{2,3},{3,2},{4,5},{5,4},{6,7},{7,6},{8,9},{9,8},{10,11... | collective-permute-start | bytes 196616 | tf_op jit(solution)/shard_map/ppermute | solution.py:719
  37.6 2.4 %collective-permute-start = (f32[4,128]{1,0:T(4,128)S(1)}, f32[4,128]{1,0:T(4,128)S(1)}, u32[]{:S(2)}, u32[]{:S(2)}) collective-permute-start(f32[4,128]{1,0:T(4,128)S(1)} %shard_map.95.facts_ref), channel_id=1, source_target_pairs={{0,1},{1,0},{2,3},{3,2},{4,5},{5,4},{6,7},{7,6},{8,9},{9,8},{10,11... | collective-permute-start | bytes 6152 | tf_op jit(solution)/shard_map/ppermute | solution.py:719
  40.0 14.7 %collective-permute-start.1 = (f32[4,128]{1,0:T(4,128)S(1)}, f32[4,128]{1,0:T(4,128)S(1)}, u32[]{:S(2)}, u32[]{:S(2)}) collective-permute-start(f32[4,128]{1,0:T(4,128)S(1)} %add.18), channel_id=1, source_target_pairs={{0,16},{1,17},{2,18},{3,19},{4,20},{5,21},{6,22},{7,23},{8,24},{9,... | collective-permute-start | bytes 6152 | tf_op jit(solution)/shard_map/ppermute | solution.py:719
  54.8 3.9 %collective-permute-start.2 = (f32[4,128]{1,0:T(4,128)S(1)}, f32[4,128]{1,0:T(4,128)S(1)}, u32[]{:S(2)}, u32[]{:S(2)}) collective-permute-start(f32[4,128]{1,0:T(4,128)S(1)} %add.19), channel_id=1, source_target_pairs={{0,2},{1,3},{2,0},{3,1},{4,6},{5,7},{6,4},{7,5},{8,10},{9,11},{10,... | collective-permute-start | bytes 6152 | tf_op jit(solution)/shard_map/ppermute | solution.py:719
  58.7 4.4 %collective-permute-start.3 = (f32[4,128]{1,0:T(4,128)S(1)}, f32[4,128]{1,0:T(4,128)S(1)}, u32[]{:S(2)}, u32[]{:S(2)}) collective-permute-start(f32[4,128]{1,0:T(4,128)S(1)} %add.20), channel_id=1, source_target_pairs={{0,32},{1,33},{2,34},{3,35},{4,36},{5,37},{6,38},{7,39},{8,40},{9,... | collective-permute-start | bytes 6152 | tf_op jit(solution)/shard_map/ppermute | solution.py:719
  63.1 3.3 %collective-permute-start.4 = (f32[4,128]{1,0:T(4,128)S(1)}, f32[4,128]{1,0:T(4,128)S(1)}, u32[]{:S(2)}, u32[]{:S(2)}) collective-permute-start(f32[4,128]{1,0:T(4,128)S(1)} %add.21), channel_id=1, source_target_pairs={{0,4},{1,5},{2,6},{3,7},{4,0},{5,1},{6,2},{7,3},{8,12},{9,13},{10,... | collective-permute-start | bytes 6152 | tf_op jit(solution)/shard_map/ppermute | solution.py:719
  66.5 6.4 %collective-permute-start.5 = (f32[4,128]{1,0:T(4,128)S(1)}, f32[4,128]{1,0:T(4,128)}, u32[]{:S(2)}, u32[]{:S(2)}) collective-permute-start(f32[4,128]{1,0:T(4,128)S(1)} %add.22), channel_id=1, source_target_pairs={{0,8},{1,9},{2,10},{3,11},{4,12},{5,13},{6,14},{7,15},{8,0},{9,1},... | collective-permute-start | bytes 6152 | tf_op jit(solution)/shard_map/ppermute | solution.py:719
  78.0 16.0 %collective-permute-start.14 = (f32[250,128]{1,0:T(8,128)S(1)}, f32[250,128]{1,0:T(8,128)S(1)}, u32[]{:S(2)}, u32[]{:S(2)}) collective-permute-start(f32[250,128]{1,0:T(8,128)S(1)} %get-tuple-element.76), channel_id=1, source_target_pairs={{0,64},{64,0},{128,192},{192,128},{1,65},{65,1},{129,193},{193,129... | collective-permute-start | bytes 384008 | tf_op jit(solution)/shard_map/ppermute | solution.py:719
  90.7 5.0 %collective-permute-start.15 = (f32[250,128]{1,0:T(8,128)S(1)}, f32[250,128]{1,0:T(8,128)S(1)}, u32[]{:S(2)}, u32[]{:S(2)}) collective-permute-start(f32[250,128]{1,0:T(8,128)S(1)} %get-tuple-element.77), channel_id=1, source_target_pairs={{0,128},{64,192},{128,0},{192,64},{1,129},{65,193},{129,1},{193,65... | collective-permute-start | bytes 384008 | tf_op jit(solution)/shard_map/ppermute | solution.py:719
  90.7 8.0 %collective-permute-start.16 = (f32[250,128]{1,0:T(8,128)S(1)}, f32[250,128]{1,0:T(8,128)S(1)}, u32[]{:S(2)}, u32[]{:S(2)}) collective-permute-start(f32[250,128]{1,0:T(8,128)S(1)} %get-tuple-element.78), channel_id=1, source_target_pairs={{0,192},{64,128},{128,64},{192,0},{1,193},{65,129},{129,65},{193,1... | collective-permute-start | bytes 384008 | tf_op jit(solution)/shard_map/ppermute | solution.py:719

commit v2 on v1

--- a/solution.py
+++ b/solution.py
@@ -507,13 +507,14 @@
     driven1_out,
     lam0_out,
     source_out,
+    u3_out,
     driven1_force,
     far,
     near,
     blocks,
     scratch,
+    u2_force,
 ):
-    u2_force = u2_out.at[pl.ds(80, 80)]
     sh = Shifts()
     odd = is_odd(slab_ref)
     incoming = Incoming(odd, far_in, near_in)
@@ -546,6 +547,11 @@
         expand(sh, stored(field), blocks)
         force(sh, blocks, stiff, scratch, out)
         put_messages(sh, odd, out, far, near, 8 * which)
+    for at in range(64):
+        f = u2_force[at]
+        if at < 16:
+            f = f + jnp.where(sh.low, 0.0, half_turn(u2_force[64 + at]))
+        u3_out[at] = 2.0 * u2_out[at] - u1_ref[at] - scale[at] * f
 
 
 def middle_kernel(
@@ -557,19 +563,12 @@
     u2_ref,
     driven1_ref,
     lam0_ref,
-    scale,
     acc,
     driven_acc,
-    u3_out,
     first,
     second,
 ):
     sh = Shifts()
-    for at in range(64):
-        f = u2_ref[80 + at]
-        if at < 16:
-            f = f + jnp.where(sh.low, 0.0, half_turn(u2_ref[144 + at]))
-        u3_out[at] = 2.0 * u2_ref[at] - u1_ref[at] - scale[at] * f
     expand(sh, stored(u1_ref), first)
     expand(sh, stored(driven1_ref), second)
     products(first, second, driven_acc, True)
@@ -805,7 +804,7 @@
     energy = across(energy, 4)
     energy = across(energy, 8)
     far, near = exchange(far, near)
-    u2, driven1, lam0, source, driven1_force, far, near = call(
+    u2, driven1, lam0, source, u3, driven1_force, far, near = call(
         step_two_kernel,
         (
             slab,
@@ -823,15 +822,15 @@
             far,
             near,
         ),
-        [vectors(160)] + [vectors(80)] * 4 + [vectors(16)] * 2,
+        [vectors(80)] * 4 + [vectors(64), vectors(80)] + [vectors(16)] * 2,
+        [vectors(125), vectors(125), vectors(80)],
+        scalars=1,
+    )
+    far, near = exchange(far, near)
+    acc, driven_acc = call(
+        middle_kernel,
+        (u0, lam2, message0, u1, lam1, u2, driven1, lam0),
         [vectors(125), vectors(125)],
-        scalars=1,
-    )
-    far, near = exchange(far, near)
-    acc, driven_acc, u3 = call(
-        middle_kernel,
-        (u0, lam2, message0, u1, lam1, u2, driven1, lam0, scale),
-        [vectors(125), vectors(125), vectors(64)],
         [vectors(125), vectors(125)],
     )
     pieces = call(

time: 120 us -> 119 us (level)
  Pallas kernels: 14.4 us -> 12.1 us
    pallas_call x13, Pallas kernels: 14.4 us -> 12.1 us  [call(): pl.pallas_call(kernel, out_shape=[jax.ShapeDtypeStruct(shape, F32) for sh...]
  transfers between devices with their start and end apart: 17 -> 17, of which waited for: 10 -> 10; matrix products, arithmetic and copies ran while one was open for 1% -> 0% of each run, Pallas kernels for 6% -> 5%
where the time goes in v2:
time: 119 us; the launch traced here: 118 us
  starting transfers between devices  57.7 us (48%)
  waiting for transfers between devices  23.7 us (20%)
  blocking collectives  20.5 us (17%)
  Pallas kernels  12.1 us (10%)
  local copies, waits for them, and re-layouts  2.4 us (2%)
  other arithmetic  1.2 us (1%)
    ppermute x17, starting transfers between devices, send(): return lax.ppermute(array, axis, pairs)  57.7 us
    ppermute x17, waiting for transfers between devices, send(): return lax.ppermute(array, axis, pairs)  23.7 us
    all_to_all x1, blocking collectives, shards(): lax.all_to_all(jnp.broadcast_to(message[None], (devices, 1, 128)), everyo...  20.5 us
    pallas_call x13, Pallas kernels, call(): pl.pallas_call(kernel, out_shape=[jax.ShapeDtypeStruct(shape, F32) for sh...  12.1 us
  transfers between devices with their start and end apart: 17, of which 10 were waited for; matrix products, arithmetic and copies ran while one was open for 0% of the time, Pallas kernels for 5%

profile of v2, /device:TPU:1, one launch (start us, length us, event | category | flops | bytes accessed | tf_op | source)
XLA Modules:
  0.0 118.4 jit_solution(784961214567878911)
XLA Ops:
  0.6 0.0 copy-start.3
  0.6 0.0 copy-start.4
  0.6 0.7 copy-done.3
  1.3 0.0 copy-done.4
  1.3 1.1 pad_maximum_fusion.1.states_ref
  2.4 0.0 copy-start.5
  2.5 0.0 copy-start.6
  2.5 0.5 shard_map.96
  3.0 1.3 %collective-permute-start.6 = (f32[17,8,128]{2,1,0:T(8,128)S(1)}, f32[17,8,128]{2,1,0:T(8,128)S(1)}, u32[]{:S(2)}, u32[]{:S(2)}) collective-permute-start(f32[17,8,128]{2,1,0:T(8,128)S(1)} %get-tuple-element.44), channel_id=1, source_target_pairs={{1,0},{2,1},{3,2},{4,3},{5,4},{6,5},{7,6},{8,7},{9,8},{10,9},{11,1... | collective-permute-start | bytes 208904 | tf_op jit(solution)/shard_map/ppermute | solution.py:718
  4.3 0.0 copy-done.7
  4.3 0.0 copy-done.5
  4.3 0.0 copy-done.6
  4.3 0.0 copy-start
  4.3 0.1 pad_maximum_fusion.fields_ref
  4.4 0.9 copy-done
  5.3 0.7 shard_map.97
  6.1 1.3 %collective-permute-start.7 = (f32[24,8,128]{2,1,0:T(8,128)S(1)}, f32[24,8,128]{2,1,0:T(8,128)S(1)}, u32[]{:S(2)}, u32[]{:S(2)}) collective-permute-start(f32[24,8,128]{2,1,0:T(8,128)S(1)} %get-tuple-element.50), channel_id=1, source_target_pairs={{1,0},{2,1},{3,2},{4,3},{5,4},{6,5},{7,6},{8,7},{9,8},{10,9},{11,1... | collective-permute-start | bytes 294920 | tf_op jit(solution)/shard_map/ppermute | solution.py:718
  7.4 1.4 %shard_map.98 = (f32[80,8,128]{2,1,0:T(8,128)S(1)}, f32[80,8,128]{2,1,0:T(8,128)S(1)}) custom-call(f32[64,8,128]{2,1,0:T(8,128)S(1)} %get-tuple-element.43.u_ref, f32[64,8,128]{2,1,0:T(8,128)S(1)} %get-tuple-element.45.lam_ref, f32[125,8,128]{2,1,0:T(8,128)S(1)} %get-tuple-element.49.stiff), custom_call_target="tpu_custom_call" | custom-call | bytes 16777216 | tf_op jit(solution)/shard_map/pallas_call | solution.py:702
  8.8 0.0 collective-permute-done.6.message.message0
  8.8 0.4 shard_map.99
  9.2 0.7 collective-permute-start.8
  9.9 6.2 %collective-permute-start.9 = (f32[16,8,128]{2,1,0:T(8,128)S(1)}, f32[16,8,128]{2,1,0:T(8,128)S(1)}, u32[]{:S(2)}, u32[]{:S(2)}) collective-permute-start(f32[16,8,128]{2,1,0:T(8,128)S(1)} %get-tuple-element.56), channel_id=1, source_target_pairs={{0,1},{1,0},{2,3},{3,2},{4,5},{5,4},{6,7},{7,6},{8,9},{9,8},{10,11... | collective-permute-start | bytes 196616 | tf_op jit(solution)/shard_map/ppermute | solution.py:718
  16.1 0.0 collective-permute-done.7.message1
  16.1 0.0 collective-permute-done.8.far_in
  16.1 1.6 %collective-permute-done.9.near_in = f32[16,8,128]{2,1,0:T(8,128)S(1)} collective-permute-done((f32[16,8,128]{2,1,0:T(8,128)S(1)}, f32[16,8,128]{2,1,0:T(8,128)S(1)}, u32[]{:S(2)}, u32[]{:S(2)}) %collective-permute-start.9) | collective-permute-done | bytes 65568 | tf_op jit(solution)/shard_map/ppermute | solution.py:718
  17.7 1.6 %shard_map.100 = (f32[80,8,128]{2,1,0:T(8,128)S(1)}, f32[80,8,128]{2,1,0:T(8,128)S(1)}, f32[80,8,128]{2,1,0:T(8,128)S(1)}, f32[80,8,128]{2,1,0:T(8,128)S(1)}, f3...) custom-call(s32[1]{0:T(128)} %bitcast.1.slab_ref, ...), custom_call_target="tpu_custom_call" | custom-call | bytes 16777216 | tf_op jit(solution)/shard_map/pallas_call | solution.py:702
  19.3 0.7 collective-permute-start.10
  20.0 7.1 %collective-permute-start.11 = (f32[16,8,128]{2,1,0:T(8,128)S(1)}, f32[16,8,128]{2,1,0:T(8,128)S(1)}, u32[]{:S(2)}, u32[]{:S(2)}) collective-permute-start(f32[16,8,128]{2,1,0:T(8,128)S(1)} %get-tuple-element.65), channel_id=1, source_target_pairs={{0,1},{1,0},{2,3},{3,2},{4,5},{5,4},{6,7},{7,6},{8,9},{9,8},{10,11... | collective-permute-start | bytes 196616 | tf_op jit(solution)/shard_map/ppermute | solution.py:718
  27.1 0.6 shard_map.101
  27.6 0.0 collective-permute-done.10.far_in
  27.7 1.1 collective-permute-done.11.near_in
  28.7 1.8 %shard_map.102 = (f32[80,8,128]{2,1,0:T(8,128)S(1)}, f32[80,8,128]{2,1,0:T(8,128)S(1)}, f32[80,8,128]{2,1,0:T(8,128)S(1)}, f32[80,8,128]{2,1,0:T(8,128)S(1)}, f3...) custom-call(s32[1]{0:T(128)} %bitcast.1.slab_ref, ...), custom_call_target="tpu_custom_call" | custom-call | bytes 16777216 | tf_op jit(solution)/shard_map/pallas_call | solution.py:702
  30.6 0.0 copy-start.1
  30.6 0.7 copy-done.1
  31.3 0.7 collective-permute-start.12
  31.9 5.8 %collective-permute-start.13 = (f32[16,8,128]{2,1,0:T(8,128)S(1)}, f32[16,8,128]{2,1,0:T(8,128)S(1)}, u32[]{:S(2)}, u32[]{:S(2)}) collective-permute-start(f32[16,8,128]{2,1,0:T(8,128)S(1)} %get-tuple-element.70), channel_id=1, source_target_pairs={{0,1},{1,0},{2,3},{3,2},{4,5},{5,4},{6,7},{7,6},{8,9},{9,8},{10,11... | collective-permute-start | bytes 196616 | tf_op jit(solution)/shard_map/ppermute | solution.py:718
  37.7 0.1 collective-permute-start
  37.8 2.3 %collective-permute-done = f32[4,128]{1,0:T(4,128)S(1)} collective-permute-done((f32[4,128]{1,0:T(4,128)S(1)}, f32[4,128]{1,0:T(4,128)S(1)}, u32[]{:S(2)}, u32[]{:S(2)}) %collective-permute-start) | collective-permute-done | bytes 2080 | tf_op jit(solution)/shard_map/ppermute | solution.py:718
  40.2 13.5 %collective-permute-start.1 = (f32[4,128]{1,0:T(4,128)S(1)}, f32[4,128]{1,0:T(4,128)S(1)}, u32[]{:S(2)}, u32[]{:S(2)}) collective-permute-start(f32[4,128]{1,0:T(4,128)S(1)} %add.18), channel_id=1, source_target_pairs={{0,16},{1,17},{2,18},{3,19},{4,20},{5,21},{6,22},{7,23},{8,24},{9,... | collective-permute-start | bytes 6152 | tf_op jit(solution)/shard_map/ppermute | solution.py:718
  53.7 1.0 collective-permute-done.1
  54.6 0.0 collective-permute-start.2
  54.6 3.9 %collective-permute-done.2 = f32[4,128]{1,0:T(4,128)S(1)} collective-permute-done((f32[4,128]{1,0:T(4,128)S(1)}, f32[4,128]{1,0:T(4,128)S(1)}, u32[]{:S(2)}, u32[]{:S(2)}) %collective-permute-start.2) | collective-permute-done | bytes 2080 | tf_op jit(solution)/shard_map/ppermute | solution.py:718
  58.6 3.3 %collective-permute-start.3 = (f32[4,128]{1,0:T(4,128)S(1)}, f32[4,128]{1,0:T(4,128)S(1)}, u32[]{:S(2)}, u32[]{:S(2)}) collective-permute-start(f32[4,128]{1,0:T(4,128)S(1)} %add.20), channel_id=1, source_target_pairs={{0,32},{1,33},{2,34},{3,35},{4,36},{5,37},{6,38},{7,39},{8,40},{9,... | collective-permute-start | bytes 6152 | tf_op jit(solution)/shard_map/ppermute | solution.py:718
  61.9 1.0 collective-permute-done.3
  62.9 0.0 collective-permute-start.4
  62.9 3.3 %collective-permute-done.4 = f32[4,128]{1,0:T(4,128)S(1)} collective-permute-done((f32[4,128]{1,0:T(4,128)S(1)}, f32[4,128]{1,0:T(4,128)S(1)}, u32[]{:S(2)}, u32[]{:S(2)}) %collective-permute-start.4) | collective-permute-done | bytes 2080 | tf_op jit(solution)/shard_map/ppermute | solution.py:718
  66.2 2.6 %collective-permute-start.5 = (f32[4,128]{1,0:T(4,128)S(1)}, f32[4,128]{1,0:T(4,128)S(1)}, u32[]{:S(2)}, u32[]{:S(2)}) collective-permute-start(f32[4,128]{1,0:T(4,128)S(1)} %add.22), channel_id=1, source_target_pairs={{0,8},{1,9},{2,10},{3,11},{4,12},{5,13},{6,14},{7,15},{8,0},{9,1},... | collective-permute-start | bytes 6152 | tf_op jit(solution)/shard_map/ppermute | solution.py:718
  68.8 3.7 %collective-permute-done.5 = f32[4,128]{1,0:T(4,128)S(1)} collective-permute-done((f32[4,128]{1,0:T(4,128)S(1)}, f32[4,128]{1,0:T(4,128)S(1)}, u32[]{:S(2)}, u32[]{:S(2)}) %collective-permute-start.5) | collective-permute-done | bytes 2080 | tf_op jit(solution)/shard_map/ppermute | solution.py:718
  72.5 2.5 %shard_map.103 = (f32[125,8,128]{2,1,0:T(8,128)S(1)}, f32[125,8,128]{2,1,0:T(8,128)S(1)}) custom-call(f32[64,8,128]{2,1,0:T(8,128)S(1)} %get-tuple-element.43.u_ref, f32[64,8,128]{2,1,0:T(8,128)S(1)} %get-tuple-element.45.lam_ref, f32[17,8,128]{2,1,0:T(8,128)S(1)} %collective-permute-done.6.message.message0, f32[80,8,128]{2,1,0:T(8,128)S(1)} %get-tuple-element.57.u1_ref, ...), custom_call_target="tpu_custom_call" | custom-call | bytes 16777216 | tf_op jit(solution)/shard_map/pallas_call | solution.py:702
  75.0 0.0 collective-permute-done.12.far_in
  75.0 0.0 collective-permute-done.13.near_in
  75.1 0.0 copy-start.2
  75.1 0.9 shard_map.104
  76.0 12.8 %collective-permute-start.14 = (f32[250,128]{1,0:T(8,128)S(1)}, f32[250,128]{1,0:T(8,128)S(1)}, u32[]{:S(2)}, u32[]{:S(2)}) collective-permute-start(f32[250,128]{1,0:T(8,128)S(1)} %get-tuple-element.76), channel_id=1, source_target_pairs={{0,64},{64,0},{128,192},{192,128},{1,65},{65,1},{129,193},{193,129... | collective-permute-start | bytes 384008 | tf_op jit(solution)/shard_map/ppermute | solution.py:718
  88.9 0.0 collective-permute-start.15
  88.9 1.7 %collective-permute-start.16 = (f32[250,128]{1,0:T(8,128)S(1)}, f32[250,128]{1,0:T(8,128)S(1)}, u32[]{:S(2)}, u32[]{:S(2)}) collective-permute-start(f32[250,128]{1,0:T(8,128)S(1)} %get-tuple-element.78), channel_id=1, source_target_pairs={{0,192},{64,128},{128,64},{192,0},{1,193},{65,129},{129,65},{193,1... | collective-permute-start | bytes 384008 | tf_op jit(solution)/shard_map/ppermute | solution.py:718
  90.6 0.6 shard_map.105.misfit
  91.2 0.0 collective-permute-done.14.b
  91.2 2.6 %collective-permute-done.15.c = f32[250,128]{1,0:T(8,128)S(1)} collective-permute-done((f32[250,128]{1,0:T(8,128)S(1)}, f32[250,128]{1,0:T(8,128)S(1)}, u32[]{:S(2)}, u32[]{:S(2)}) %collective-permute-start.15) | collective-permute-done | bytes 128032 | tf_op jit(solution)/shard_map/ppermute | solution.py:718
  93.8 3.1 %collective-permute-done.16.d = f32[250,128]{1,0:T(8,128)S(1)} collective-permute-done((f32[250,128]{1,0:T(8,128)S(1)}, f32[250,128]{1,0:T(8,128)S(1)}, u32[]{:S(2)}, u32[]{:S(2)}) %collective-permute-start.16) | collective-permute-done | bytes 128032 | tf_op jit(solution)/shard_map/ppermute | solution.py:718
  96.9 0.1 shard_map.106
  97.0 0.1 broadcast_in_dim.9
  97.1 20.5 %all_to_all.5 = f32[256,1,128]{2,1,0:T(1,128)S(1)} all-to-all(f32[256,1,128]{2,1,0:T(1,128)S(1)} %broadcast_in_dim.9), channel_id=1, replica_groups=mesh['event'=4,'space'=64] {'event','space'}, dimensions={0} | all-to-all | bytes 262144 | tf_op jit(solution)/shard_map/all_to_all | solution.py:871
  117.6 0.8 shard_map.107
  (9 shorter events, 0.0 us)
Async XLA Ops:
  0.6 0.7 copy-start.3
  0.6 0.7 copy-start.4
  1.3 3.0 %copy-start.7 = (f32[1,8,16,512]{3,2,1,0:T(8,128)S(1)}, f32[1,8,16,512]{3,2,1,0:T(8,128)}, u32[]{:S(2)}) copy-start(f32[1,8,16,512]{3,2,1,0:T(8,128)} %param.9) | copy-start | bytes 786436
  2.4 1.8 %copy-start.5 = (f32[8,16,512]{2,1,0:T(8,128)S(1)}, f32[8,16,512]{2,1,0:T(8,128)}, u32[]{:S(2)}) copy-start(f32[8,16,512]{2,1,0:T(8,128)} %param.13) | copy-start | bytes 786436
  2.5 1.8 %copy-start.6 = (f32[1,8,16,512]{3,2,1,0:T(8,128)S(1)}, f32[1,8,16,512]{3,2,1,0:T(8,128)}, u32[]{:S(2)}) copy-start(f32[1,8,16,512]{3,2,1,0:T(8,128)} %param.11) | copy-start | bytes 786436
  3.0 5.8 %collective-permute-start.6 = (f32[17,8,128]{2,1,0:T(8,128)S(1)}, f32[17,8,128]{2,1,0:T(8,128)S(1)}, u32[]{:S(2)}, u32[]{:S(2)}) collective-permute-start(f32[17,8,128]{2,1,0:T(8,128)S(1)} %get-tuple-element.44), channel_id=1, source_target_pairs={{1,0},{2,1},{3,2},{4,3},{5,4},{6,5},{7,6},{8,7},{9,8},{10,9},{11,1... | collective-permute-start | bytes 208904 | tf_op jit(solution)/shard_map/ppermute | solution.py:718
  4.3 1.0 copy-start
  6.1 10.0 %collective-permute-start.7 = (f32[24,8,128]{2,1,0:T(8,128)S(1)}, f32[24,8,128]{2,1,0:T(8,128)S(1)}, u32[]{:S(2)}, u32[]{:S(2)}) collective-permute-start(f32[24,8,128]{2,1,0:T(8,128)S(1)} %get-tuple-element.50), channel_id=1, source_target_pairs={{1,0},{2,1},{3,2},{4,3},{5,4},{6,5},{7,6},{8,7},{9,8},{10,9},{11,1... | collective-permute-start | bytes 294920 | tf_op jit(solution)/shard_map/ppermute | solution.py:718
  9.2 6.8 %collective-permute-start.8 = (f32[16,8,128]{2,1,0:T(8,128)S(1)}, f32[16,8,128]{2,1,0:T(8,128)S(1)}, u32[]{:S(2)}, u32[]{:S(2)}) collective-permute-start(f32[16,8,128]{2,1,0:T(8,128)S(1)} %get-tuple-element.55), channel_id=1, source_target_pairs={{1,2},{2,1},{3,4},{4,3},{5,6},{6,5},{7,8},{8,7},{9,10},{10,9},{11,... | collective-permute-start | bytes 196616 | tf_op jit(solution)/shard_map/ppermute | solution.py:718
  9.9 7.8 %collective-permute-start.9 = (f32[16,8,128]{2,1,0:T(8,128)S(1)}, f32[16,8,128]{2,1,0:T(8,128)S(1)}, u32[]{:S(2)}, u32[]{:S(2)}) collective-permute-start(f32[16,8,128]{2,1,0:T(8,128)S(1)} %get-tuple-element.56), channel_id=1, source_target_pairs={{0,1},{1,0},{2,3},{3,2},{4,5},{5,4},{6,7},{7,6},{8,9},{9,8},{10,11... | collective-permute-start | bytes 196616 | tf_op jit(solution)/shard_map/ppermute | solution.py:718
  19.3 8.3 %collective-permute-start.10 = (f32[16,8,128]{2,1,0:T(8,128)S(1)}, f32[16,8,128]{2,1,0:T(8,128)S(1)}, u32[]{:S(2)}, u32[]{:S(2)}) collective-permute-start(f32[16,8,128]{2,1,0:T(8,128)S(1)} %get-tuple-element.64), channel_id=1, source_target_pairs={{1,2},{2,1},{3,4},{4,3},{5,6},{6,5},{7,8},{8,7},{9,10},{10,9},{11,... | collective-permute-start | bytes 196616 | tf_op jit(solution)/shard_map/ppermute | solution.py:718
  20.0 8.7 %collective-permute-start.11 = (f32[16,8,128]{2,1,0:T(8,128)S(1)}, f32[16,8,128]{2,1,0:T(8,128)S(1)}, u32[]{:S(2)}, u32[]{:S(2)}) collective-permute-start(f32[16,8,128]{2,1,0:T(8,128)S(1)} %get-tuple-element.65), channel_id=1, source_target_pairs={{0,1},{1,0},{2,3},{3,2},{4,5},{5,4},{6,7},{7,6},{8,9},{9,8},{10,11... | collective-permute-start | bytes 196616 | tf_op jit(solution)/shard_map/ppermute | solution.py:718
  30.6 0.7 copy-start.1
  31.3 43.8 %collective-permute-start.12 = (f32[16,8,128]{2,1,0:T(8,128)S(1)}, f32[16,8,128]{2,1,0:T(8,128)S(1)}, u32[]{:S(2)}, u32[]{:S(2)}) collective-permute-start(f32[16,8,128]{2,1,0:T(8,128)S(1)} %get-tuple-element.69), channel_id=1, source_target_pairs={{1,2},{2,1},{3,4},{4,3},{5,6},{6,5},{7,8},{8,7},{9,10},{10,9},{11,... | collective-permute-start | bytes 196616 | tf_op jit(solution)/shard_map/ppermute | solution.py:718
  31.9 43.1 %collective-permute-start.13 = (f32[16,8,128]{2,1,0:T(8,128)S(1)}, f32[16,8,128]{2,1,0:T(8,128)S(1)}, u32[]{:S(2)}, u32[]{:S(2)}) collective-permute-start(f32[16,8,128]{2,1,0:T(8,128)S(1)} %get-tuple-element.70), channel_id=1, source_target_pairs={{0,1},{1,0},{2,3},{3,2},{4,5},{5,4},{6,7},{7,6},{8,9},{9,8},{10,11... | collective-permute-start | bytes 196616 | tf_op jit(solution)/shard_map/ppermute | solution.py:718
  37.7 2.4 %collective-permute-start = (f32[4,128]{1,0:T(4,128)S(1)}, f32[4,128]{1,0:T(4,128)S(1)}, u32[]{:S(2)}, u32[]{:S(2)}) collective-permute-start(f32[4,128]{1,0:T(4,128)S(1)} %shard_map.95.facts_ref), channel_id=1, source_target_pairs={{0,1},{1,0},{2,3},{3,2},{4,5},{5,4},{6,7},{7,6},{8,9},{9,8},{10,11... | collective-permute-start | bytes 6152 | tf_op jit(solution)/shard_map/ppermute | solution.py:718
  40.2 14.5 %collective-permute-start.1 = (f32[4,128]{1,0:T(4,128)S(1)}, f32[4,128]{1,0:T(4,128)S(1)}, u32[]{:S(2)}, u32[]{:S(2)}) collective-permute-start(f32[4,128]{1,0:T(4,128)S(1)} %add.18), channel_id=1, source_target_pairs={{0,16},{1,17},{2,18},{3,19},{4,20},{5,21},{6,22},{7,23},{8,24},{9,... | collective-permute-start | bytes 6152 | tf_op jit(solution)/shard_map/ppermute | solution.py:718
  54.6 3.9 %collective-permute-start.2 = (f32[4,128]{1,0:T(4,128)S(1)}, f32[4,128]{1,0:T(4,128)S(1)}, u32[]{:S(2)}, u32[]{:S(2)}) collective-permute-start(f32[4,128]{1,0:T(4,128)S(1)} %add.19), channel_id=1, source_target_pairs={{0,2},{1,3},{2,0},{3,1},{4,6},{5,7},{6,4},{7,5},{8,10},{9,11},{10,... | collective-permute-start | bytes 6152 | tf_op jit(solution)/shard_map/ppermute | solution.py:718
  58.6 4.3 %collective-permute-start.3 = (f32[4,128]{1,0:T(4,128)S(1)}, f32[4,128]{1,0:T(4,128)S(1)}, u32[]{:S(2)}, u32[]{:S(2)}) collective-permute-start(f32[4,128]{1,0:T(4,128)S(1)} %add.20), channel_id=1, source_target_pairs={{0,32},{1,33},{2,34},{3,35},{4,36},{5,37},{6,38},{7,39},{8,40},{9,... | collective-permute-start | bytes 6152 | tf_op jit(solution)/shard_map/ppermute | solution.py:718
  62.9 3.3 %collective-permute-start.4 = (f32[4,128]{1,0:T(4,128)S(1)}, f32[4,128]{1,0:T(4,128)S(1)}, u32[]{:S(2)}, u32[]{:S(2)}) collective-permute-start(f32[4,128]{1,0:T(4,128)S(1)} %add.21), channel_id=1, source_target_pairs={{0,4},{1,5},{2,6},{3,7},{4,0},{5,1},{6,2},{7,3},{8,12},{9,13},{10,... | collective-permute-start | bytes 6152 | tf_op jit(solution)/shard_map/ppermute | solution.py:718
  66.2 6.3 %collective-permute-start.5 = (f32[4,128]{1,0:T(4,128)S(1)}, f32[4,128]{1,0:T(4,128)S(1)}, u32[]{:S(2)}, u32[]{:S(2)}) collective-permute-start(f32[4,128]{1,0:T(4,128)S(1)} %add.22), channel_id=1, source_target_pairs={{0,8},{1,9},{2,10},{3,11},{4,12},{5,13},{6,14},{7,15},{8,0},{9,1},... | collective-permute-start | bytes 6152 | tf_op jit(solution)/shard_map/ppermute | solution.py:718
  75.1 15.5 %copy-start.2 = (f32[64,8,128]{2,1,0:T(8,128)S(1)}, f32[64,8,128]{2,1,0:T(8,128)}, u32[]{:S(2)}) copy-start(f32[64,8,128]{2,1,0:T(8,128)} %copy-done.1) | copy-start | bytes 786436
  76.0 15.2 %collective-permute-start.14 = (f32[250,128]{1,0:T(8,128)S(1)}, f32[250,128]{1,0:T(8,128)S(1)}, u32[]{:S(2)}, u32[]{:S(2)}) collective-permute-start(f32[250,128]{1,0:T(8,128)S(1)} %get-tuple-element.76), channel_id=1, source_target_pairs={{0,64},{64,0},{128,192},{192,128},{1,65},{65,1},{129,193},{193,129... | collective-permute-start | bytes 384008 | tf_op jit(solution)/shard_map/ppermute | solution.py:718
  88.9 5.0 %collective-permute-start.15 = (f32[250,128]{1,0:T(8,128)S(1)}, f32[250,128]{1,0:T(8,128)S(1)}, u32[]{:S(2)}, u32[]{:S(2)}) collective-permute-start(f32[250,128]{1,0:T(8,128)S(1)} %get-tuple-element.77), channel_id=1, source_target_pairs={{0,128},{64,192},{128,0},{192,64},{1,129},{65,193},{129,1},{193,65... | collective-permute-start | bytes 384008 | tf_op jit(solution)/shard_map/ppermute | solution.py:718
  88.9 8.0 %collective-permute-start.16 = (f32[250,128]{1,0:T(8,128)S(1)}, f32[250,128]{1,0:T(8,128)S(1)}, u32[]{:S(2)}, u32[]{:S(2)}) collective-permute-start(f32[250,128]{1,0:T(8,128)S(1)} %get-tuple-element.78), channel_id=1, source_target_pairs={{0,192},{64,128},{128,64},{192,0},{1,193},{65,129},{129,65},{193,1... | collective-permute-start | bytes 384008 | tf_op jit(solution)/shard_map/ppermute | solution.py:718
